TPU v7x, 256 devices: a whole 4x4x8 slice. The times are simulated.
256 devices in a mesh: inner: 8 (over y, core), outer: 32 (over z, x).
Axes of the slice: x: 4, y: 4, z: 8, core: 2. Of those that a mesh axis runs over, the one named last changes fastest.
Arguments:
- query_rows: bfloat16 [131072, 512], P(('outer', 'inner')), may hold values from -6 to 6
- key_rows: bfloat16 [131072, 512], P(('outer', 'inner')), may hold values from -6 to 6
- value_rows: bfloat16 [131072, 512], P(('outer', 'inner')), may hold values from -6 to 6
- level_ids: int32 [131072], P(('outer', 'inner')), may hold values from 0 to 15
- level_table: float32 [16, 16, 4], replicated, may hold values from 0.1 to 1
Outputs:
- attended: bfloat16 [131072, 512], P(('outer', 'inner'))
All inputs are finite; a program needn't handle non-finite values.
Results may differ from a plain program's by a relative error of at most 0.0049.
Values sent between devices are 32-bit elements; how exact they have to be, the bound alone decides.
A program may use at most 64 MiB of HBM per device.

v0:
```python
import jax
import jax.numpy as jnp
import numpy as np
from jax import lax
from jax.sharding import PartitionSpec as P

HEADS = 4
HD = 128
SPAN = 128
LEVELS = 16


norm_eps = 1e-06


def sent_to_all(value, axis):
    copies = jnp.broadcast_to(value, (lax.axis_size(axis), *value.shape))
    return lax.all_to_all(copies, axis, split_axis=0, concat_axis=0, tiled=True)


def joined_along(tiles, dim):
    tiles = jnp.moveaxis(tiles, 0, dim)
    dims = tiles.shape
    return tiles.reshape(*dims[:dim], dims[dim] * dims[dim + 1], *dims[dim + 2 :])


def gathered_copies(value, axis, dim):
    tiles = sent_to_all(value, axis)
    return joined_along(tiles, dim)


def from_partner(value, axis, apart):
    return lax.ppermute(value, axis, [(i, i ^ 1 << apart) for i in range(lax.axis_size(axis))])


def exclusive_prefix(stacked):
    zeros = jnp.zeros((1,) + stacked.shape[1:], jnp.float32)
    return jnp.concatenate([zeros, jnp.cumsum(stacked, axis=0)], axis=0)


def pick_left(gathered, own_index, level_bits):
    prefix = exclusive_prefix(gathered)
    result = []
    for bit_pos in range(level_bits):
        upper = own_index >> bit_pos << bit_pos
        lower = own_index >> bit_pos + 1 << bit_pos + 1
        active = (own_index >> bit_pos & 1).astype(jnp.float32)
        high_part = lax.dynamic_index_in_dim(prefix, upper, 0, keepdims=False)
        low_part = lax.dynamic_index_in_dim(prefix, lower, 0, keepdims=False)
        result.append((high_part - low_part) * active)
    return result


def local_output(query_rows, key_blocks, value_blocks, span_states, weights_tok, cross_states):
    token_count = query_rows.shape[0]
    span_count = token_count // SPAN
    level_bits = span_count.bit_length() - 1
    query_blocks = query_rows.reshape(span_count, SPAN, HEADS, HD)
    level_blocks = weights_tok.reshape(span_count, SPAN, LEVELS, HEADS)
    scores = jnp.einsum(
        "cthd,cshd->chts", query_blocks, key_blocks, preferred_element_type=jnp.float32
    )
    position = jnp.arange(SPAN, dtype=jnp.int32)
    causal = position[:, None] >= position[None, :]
    scale_now = jnp.transpose(level_blocks[:, :, 0, :], (0, 2, 1))[..., None]
    weighted = jnp.where(causal, scores * scale_now, 0.0).astype(jnp.bfloat16)
    unnormed = jnp.einsum(
        "chts,cshd->cthd", weighted, value_blocks, preferred_element_type=jnp.float32
    )
    prefix = exclusive_prefix(span_states)
    span_ids = np.arange(span_count)
    for bit_pos in range(level_bits):
        upper = span_ids >> bit_pos << bit_pos
        lower = span_ids >> bit_pos + 1 << bit_pos + 1
        active = jnp.asarray((span_ids >> bit_pos & 1).astype(np.float32))
        left_block = (prefix[upper] - prefix[lower]) * active[:, None, None, None]
        left_block = left_block.astype(jnp.bfloat16)
        partial_out = jnp.einsum(
            "cthd,chde->cthe", query_blocks, left_block, preferred_element_type=jnp.float32
        )
        unnormed = unnormed + level_blocks[:, :, 1 + bit_pos, :, None] * partial_out
    unnormed = unnormed.reshape(token_count, HEADS, HD)
    query_heads = query_rows.reshape(token_count, HEADS, HD)
    for bit_pos in range(len(cross_states)):
        partial_out = jnp.einsum(
            "thd,hde->the", query_heads, cross_states[bit_pos], preferred_element_type=jnp.float32
        )
        unnormed = unnormed + weights_tok[:, 1 + level_bits + bit_pos, :, None] * partial_out
    mean_square = jnp.mean(unnormed * unnormed, axis=-1, keepdims=True)
    normed = unnormed * lax.rsqrt(mean_square + norm_eps)
    return normed.reshape(token_count, HEADS * HD).astype(jnp.bfloat16)


def on_device(query_rows, key_rows, value_rows, level_ids, level_table):
    token_count = query_rows.shape[0]
    classes = level_table.shape[0]
    onehot = (level_ids[:, None] == jnp.arange(classes, dtype=jnp.int32)[None, :]).astype(
        jnp.float32
    )
    table_flat = level_table.reshape(classes, -1)
    weights_tok = jnp.sum(onehot[:, :, None] * table_flat[None, :, :], axis=1).reshape(
        token_count, LEVELS, HEADS
    )
    span_count = token_count // SPAN
    key_blocks = key_rows.reshape(span_count, SPAN, HEADS, HD)
    value_blocks = value_rows.reshape(span_count, SPAN, HEADS, HD)
    span_states = jnp.einsum(
        "cthd,cthe->chde", key_blocks, value_blocks, preferred_element_type=jnp.float32
    )
    group_state = jnp.sum(span_states, axis=0)
    inner_index = lax.axis_index("inner")
    inner_bits = lax.axis_size("inner").bit_length() - 1
    gathered = gathered_copies(group_state[None], "inner", 0)
    left_states = pick_left(gathered, inner_index, inner_bits)
    group_state = jnp.sum(gathered, axis=0)
    outer_index = lax.axis_index("outer")
    outer_bits = lax.axis_size("outer").bit_length() - 1
    for bit_pos in range(outer_bits):
        partner = from_partner(group_state, "outer", bit_pos)
        active = (outer_index >> bit_pos & 1).astype(jnp.float32)
        left_states.append(partner * active)
        group_state = group_state + partner
    cross_states = [state.astype(jnp.bfloat16) for state in left_states]
    return local_output(
        query_rows, key_blocks, value_blocks, span_states, weights_tok, cross_states
    )


def solution(mesh):
    in_specs = (
        P(("outer", "inner"), None),
        P(("outer", "inner"), None),
        P(("outer", "inner"), None),
        P(("outer", "inner")),
        P(),
    )
    out_specs = P(("outer", "inner"), None)
    return jax.shard_map(
        on_device, mesh=mesh, in_specs=in_specs, out_specs=out_specs, check_vma=False
    )
```

profile of v0, /device:TPU:6, one launch (start us, length us, event | category | flops | bytes accessed | tf_op | source)
XLA Modules:
  0.0 90.7 jit_solution(10770132017866575474)
XLA Ops:
  0.0 1.2 %reshape.80 = bf16[4,128,4,128]{3,2,1,0:T(4,128)(2,1)S(1)} reshape(bf16[512,512]{1,0:T(8,128)(2,1)} %param.16) | data formatting | bytes 1048576 | tf_op jit(solution)/shard_map/reshape | solution.py:105
  1.7 1.3 %fusion.78 = (f32[4,128,128]{2,1,0:T(8,128)S(1)}, f32[4,4,128,128]{3,2,1,0:T(8,128)}) fusion(bf16[4,128,4,128]{1,3,2,0:T(8,128)(2,1)S(1)} %copy.82, bf16[4,128,4,128]{3,2,1,0:T(4,128)(2,1)S(1)} %reshape.81), kind=kOutput, calls=%fused_computation.121 | convolution fusion | flops 67305472 | bytes 2359296 | tf_op jit(solution)/shard_map/cthd,cthe->chde/dot_general | solution.py:107
  3.2 1.6 %broadcast_in_dim.39 = f32[8,1,4,128,128]{3,4,2,1,0:T(8,128)} broadcast(f32[4,128,128]{1,2,0:T(8,128)S(1)} %copy.88), dimensions={2,3,4} | broadcast | bytes 2359296 | tf_op jit(solution)/shard_map/broadcast_in_dim | solution.py:17
  4.7 4.6 %all-to-all-start = ((f32[8,1,4,128,128]{3,4,2,1,0:T(8,128)}), f32[8,1,4,128,128]{3,4,2,1,0:T(8,128)S(1)}, u32[]{:S(2)}, u32[]{:S(2)}) async-start(f32[8,1,4,128,128]{3,4,2,1,0:T(8,128)} %broadcast_in_dim.39), calls=%async_computation | async-start | bytes 4194304 | tf_op jit(solution)/shard_map/all_to_all | solution.py:18
  10.0 1.3 %fusion.79 = f32[4,4,128,128]{3,2,1,0:T(8,128)S(1)} fusion(f32[4,4,128,128]{3,2,1,0:T(8,128)} %get-tuple-element.17), kind=kOutput, calls=%fused_computation.122 | output fusion | flops 786432 | bytes 2097152 | tf_op jit(solution)/shard_map/jit(cumsum)/reduce_window_sum | solution.py:38
  11.4 1.2 %concatenate.6 = f32[5,4,128,128]{3,2,1,0:T(8,128)} pad(f32[4,4,128,128]{3,2,1,0:T(8,128)S(1)} %fusion.79, f32[]{:T(128)} %constant.49.clone.1), padding=1_0x0_0x0_0x0_0 | pad | bytes 2359300 | tf_op jit(solution)/shard_map/concatenate | solution.py:38
  12.6 2.9 %gather_fusion.1 = f32[4,4,128,128]{3,2,1,0:T(8,128)} fusion(f32[5,4,128,128]{3,2,1,0:T(8,128)} %concatenate.6, s32[1024]{0:T(1024)S(1)} %pad_clamp_fusion.1), kind=kCustom, calls=%fused_computation.1 | custom fusion | bytes 2097168 | tf_op jit(solution)/shard_map/gather | solution.py:76
  15.5 2.9 %gather_fusion = f32[4,4,128,128]{3,2,1,0:T(8,128)} fusion(f32[5,4,128,128]{3,2,1,0:T(8,128)} %concatenate.6, s32[1024]{0:T(1024)S(1)} %pad_clamp_fusion.2), kind=kCustom, calls=%fused_computation | custom fusion | bytes 2097168 | tf_op jit(solution)/shard_map/gather | solution.py:76
  18.4 2.9 %gather_fusion.2 = f32[4,4,128,128]{3,2,1,0:T(8,128)} fusion(f32[5,4,128,128]{3,2,1,0:T(8,128)} %concatenate.6, s32[1024]{0:T(1024)S(1)} %pad_clamp_fusion), kind=kCustom, calls=%fused_computation.2 | custom fusion | bytes 2097168 | tf_op jit(solution)/shard_map/gather | solution.py:76
  21.3 2.7 %convolution_bitcast_fusion.10 = f32[4,128,4,128]{3,1,2,0:T(8,128)} fusion(bf16[4,128,4,128]{1,3,2,0:T(8,128)(2,1)} %copy-done.4, f32[4,4,128]{2,1,0:T(4,128)S(1)} %copy.79, pred[128,128]{1,0:T(8,128)(4,1)S(1)} %iota_compare_fusion, bf16[4,128,4,128]{3,2,1,0:T(4,128)(2,1)} %copy-done.5, bf16[4,128,4,128]{3,2,1,0:T(4,128)(2,1)S(1)} %reshape.79), kind=kOutput, calls=%fused_computation.40 | convolution fusion | flops 135004160 | bytes 2646016 | tf_op jit(solution)/shard_map/chts,cshd->cthd/dot_general | solution.py:67
  24.0 2.4 %fusion.5 = f32[4,128,4,128]{3,1,2,0:T(8,128)S(1)} fusion(f32[4,128,4,128]{3,1,2,0:T(8,128)} %convolution_bitcast_fusion.10, f32[4,4,128,128]{3,2,1,0:T(8,128)} %gather_fusion, f32[4,4,128,128]{3,2,1,0:T(8,128)} %gather_fusion.1, f32[4]{0:T(128)S(1)} %copy-done.10, f32[4,128,4]{1,2,0:T(4,128)S(1)} %copy.81, bf16[4,128,4,128]{3,2,1,0:T(4,128)(2,1)S(1)} %reshape.79), kind=kOutput, calls=%fused_computation.15 | convolution fusion | flops 68419584 | bytes 4726800 | tf_op jit(solution)/shard_map/cthd,chde->cthe/dot_general | solution.py:78
  27.2 1.1 %copy.87 = f32[4,128,4,128]{3,1,0,2:T(8,128)} copy(f32[4,128,4,128]{3,1,2,0:T(8,128)S(1)} %fusion.3) | data formatting | bytes 2097152 | tf_op jit(solution)/shard_map/add | solution.py:81
  28.2 2.5 %copy.90 = f32[512,4,128]{0,2,1:T(8,128)} copy(f32[512,4,128]{2,0,1:T(8,128)} %bitcast.152) | data formatting | bytes 2097152 | tf_op jit(solution)/shard_map/reshape | solution.py:82
  30.8 5.7 %all-to-all-done = f32[8,1,4,128,128]{3,4,2,1,0:T(8,128)S(1)} async-done(((f32[8,1,4,128,128]{3,4,2,1,0:T(8,128)}), f32[8,1,4,128,128]{3,4,2,1,0:T(8,128)S(1)}, u32[]{:S(2)}, u32[]{:S(2)}) %all-to-all-start) | async-done | bytes 2097184 | tf_op jit(solution)/shard_map/all_to_all | solution.py:18
  37.6 1.9 %fusion = f32[8,4,128,128]{2,3,1,0:T(8,128)S(1)} fusion(f32[8,1,4,128,128]{3,4,2,1,0:T(8,128)S(1)} %all-to-all-done), kind=kOutput, calls=%fused_computation.7 | output fusion | flops 3670016 | bytes 4194304 | tf_op jit(solution)/shard_map/jit(cumsum)/reduce_window_sum | solution.py:38
  40.5 4.0 %collective-permute-done = f32[4,128,128]{1,2,0:T(8,128)S(1)} collective-permute-done((f32[4,128,128]{1,2,0:T(8,128)S(1)}, f32[4,128,128]{1,2,0:T(8,128)S(1)}, u32[]{:S(2)}, u32[]{:S(2)}) %collective-permute-start) | collective-permute-done | bytes 262176 | tf_op jit(solution)/shard_map/ppermute | solution.py:33
  44.5 1.5 %collective-permute-start.1 = (f32[4,128,128]{1,2,0:T(8,128)S(1)}, f32[4,128,128]{1,2,0:T(8,128)S(1)}, u32[]{:S(2)}, u32[]{:S(2)}) collective-permute-start(f32[4,128,128]{1,2,0:T(8,128)S(1)} %add.98), channel_id=1, source_target_pairs={{0,2},{1,3},{2,0},{3,1},{4,6},{5,7},{6,4},{7,5},{8,10},{9,11},{10,... | collective-permute-start | bytes 786440 | tf_op jit(solution)/shard_map/ppermute | solution.py:33
  46.4 6.7 %collective-permute-done.1 = f32[4,128,128]{1,2,0:T(8,128)S(1)} collective-permute-done((f32[4,128,128]{1,2,0:T(8,128)S(1)}, f32[4,128,128]{1,2,0:T(8,128)S(1)}, u32[]{:S(2)}, u32[]{:S(2)}) %collective-permute-start.1) | collective-permute-done | bytes 262176 | tf_op jit(solution)/shard_map/ppermute | solution.py:33
  53.1 2.0 %collective-permute-start.2 = (f32[4,128,128]{1,2,0:T(8,128)S(1)}, f32[4,128,128]{1,2,0:T(8,128)S(1)}, u32[]{:S(2)}, u32[]{:S(2)}) collective-permute-start(f32[4,128,128]{1,2,0:T(8,128)S(1)} %add.100), channel_id=1, source_target_pairs={{0,4},{1,5},{2,6},{3,7},{4,0},{5,1},{6,2},{7,3},{8,12},{9,13},{10,... | collective-permute-start | bytes 786440 | tf_op jit(solution)/shard_map/ppermute | solution.py:33
  55.4 4.2 %collective-permute-done.2 = f32[4,128,128]{1,2,0:T(8,128)S(1)} collective-permute-done((f32[4,128,128]{1,2,0:T(8,128)S(1)}, f32[4,128,128]{1,2,0:T(8,128)S(1)}, u32[]{:S(2)}, u32[]{:S(2)}) %collective-permute-start.2) | collective-permute-done | bytes 262176 | tf_op jit(solution)/shard_map/ppermute | solution.py:33
  59.6 3.8 %collective-permute-start.3 = (f32[4,128,128]{1,2,0:T(8,128)S(1)}, f32[4,128,128]{1,2,0:T(8,128)S(1)}, u32[]{:S(2)}, u32[]{:S(2)}) collective-permute-start(f32[4,128,128]{1,2,0:T(8,128)S(1)} %add.102), channel_id=1, source_target_pairs={{0,8},{1,9},{2,10},{3,11},{4,12},{5,13},{6,14},{7,15},{8,0},{9,1},... | collective-permute-start | bytes 786440 | tf_op jit(solution)/shard_map/ppermute | solution.py:33
  63.6 8.2 %collective-permute-done.3 = f32[4,128,128]{1,2,0:T(8,128)S(1)} collective-permute-done((f32[4,128,128]{1,2,0:T(8,128)S(1)}, f32[4,128,128]{1,2,0:T(8,128)S(1)}, u32[]{:S(2)}, u32[]{:S(2)}) %collective-permute-start.3) | collective-permute-done | bytes 262176 | tf_op jit(solution)/shard_map/ppermute | solution.py:33
  71.9 6.5 %collective-permute-start.4 = (f32[4,128,128]{1,2,0:T(8,128)S(1)}, f32[4,128,128]{1,2,0:T(8,128)S(1)}, u32[]{:S(2)}, u32[]{:S(2)}) collective-permute-start(f32[4,128,128]{1,2,0:T(8,128)S(1)} %add.104), channel_id=1, source_target_pairs={{0,16},{1,17},{2,18},{3,19},{4,20},{5,21},{6,22},{7,23},{8,24},{9,... | collective-permute-start | bytes 786440 | tf_op jit(solution)/shard_map/ppermute | solution.py:33
  78.7 10.4 %collective-permute-done.4 = f32[4,128,128]{1,2,0:T(8,128)S(1)} collective-permute-done((f32[4,128,128]{1,2,0:T(8,128)S(1)}, f32[4,128,128]{1,2,0:T(8,128)S(1)}, u32[]{:S(2)}, u32[]{:S(2)}) %collective-permute-start.4) | collective-permute-done | bytes 262176 | tf_op jit(solution)/shard_map/ppermute | solution.py:33
  (63 shorter events, 6.7 us)
Async XLA Ops:
  0.0 1.5 %copy-start.6 = (bf16[512,512]{1,0:T(8,128)(2,1)S(1)}, bf16[512,512]{1,0:T(8,128)(2,1)}, u32[]{:S(2)}) copy-start(bf16[512,512]{1,0:T(8,128)(2,1)} %param.17) | copy-start | bytes 1572868
  1.5 3.2 %copy-start.4 = (bf16[4,128,4,128]{1,3,2,0:T(8,128)(2,1)}, bf16[4,128,4,128]{1,3,2,0:T(8,128)(2,1)S(1)}, u32[]{:S(2)}) copy-start(bf16[4,128,4,128]{1,3,2,0:T(8,128)(2,1)S(1)} %copy.82) | copy-start | bytes 1572868
  1.7 1.5 %copy-start.5 = (bf16[4,128,4,128]{3,2,1,0:T(4,128)(2,1)}, bf16[4,128,4,128]{3,2,1,0:T(4,128)(2,1)S(1)}, u32[]{:S(2)}) copy-start(bf16[4,128,4,128]{3,2,1,0:T(4,128)(2,1)S(1)} %reshape.81) | copy-start | bytes 1572868
  4.7 4.6 %copy-start.7 = (f32[16,16,4]{1,2,0:T(4,128)S(1)}, f32[16,16,4]{1,2,0:T(4,128)}, u32[]{:S(2)}) copy-start(f32[16,16,4]{1,2,0:T(4,128)} %param.19) | copy-start | bytes 12292
  4.7 4.8 %copy-start.8 = (s32[512]{0:T(512)S(1)}, s32[512]{0:T(512)}, u32[]{:S(2)}) copy-start(s32[512]{0:T(512)} %param.18) | copy-start | bytes 6148
  4.7 5.2 %copy-start = (bf16[512,512]{1,0:T(8,128)(2,1)S(1)}, bf16[512,512]{1,0:T(8,128)(2,1)}, u32[]{:S(2)}) copy-start(bf16[512,512]{1,0:T(8,128)(2,1)} %param.15) | copy-start | bytes 1572868
  4.7 31.8 %all-to-all-start = ((f32[8,1,4,128,128]{3,4,2,1,0:T(8,128)}), f32[8,1,4,128,128]{3,4,2,1,0:T(8,128)S(1)}, u32[]{:S(2)}, u32[]{:S(2)}) async-start(f32[8,1,4,128,128]{3,4,2,1,0:T(8,128)} %broadcast_in_dim.39), calls=%async_computation | async-start | bytes 4194304 | tf_op jit(solution)/shard_map/all_to_all | solution.py:18
  10.0 2.5 %copy-start.11 = (s32[4]{0:T(128)S(1)}, s32[4]{0:T(128)}, u32[]{:S(2)}) copy-start(s32[4]{0:T(128)} %constant.72) | copy-start | bytes 52
  18.4 5.6 %copy-start.10 = (f32[4]{0:T(128)S(1)}, f32[4]{0:T(128)}, u32[]{:S(2)}) copy-start(f32[4]{0:T(128)} %constant.62.clone) | copy-start | bytes 52
  24.0 2.4 %copy-start.1 = (f32[4,4,128,128]{3,2,1,0:T(8,128)S(1)}, f32[4,4,128,128]{3,2,1,0:T(8,128)}, u32[]{:S(2)}) copy-start(f32[4,4,128,128]{3,2,1,0:T(8,128)} %gather_fusion.1) | copy-start | bytes 3145732
  24.0 2.5 %copy-start.2 = (f32[4,4,128,128]{3,2,1,0:T(8,128)S(1)}, f32[4,4,128,128]{3,2,1,0:T(8,128)}, u32[]{:S(2)}) copy-start(f32[4,4,128,128]{3,2,1,0:T(8,128)} %gather_fusion.2) | copy-start | bytes 3145732
  24.0 2.5 %copy-start.9 = (f32[4]{0:T(128)S(1)}, f32[4]{0:T(128)}, u32[]{:S(2)}) copy-start(f32[4]{0:T(128)} %constant.65.clone) | copy-start | bytes 52
  36.6 2.9 %copy-start.3 = (f32[512,4,128]{0,2,1:T(8,128)S(1)}, f32[512,4,128]{0,2,1:T(8,128)}, u32[]{:S(2)}) copy-start(f32[512,4,128]{0,2,1:T(8,128)} %copy.90) | copy-start | bytes 3145732
  36.7 7.8 %collective-permute-start = (f32[4,128,128]{1,2,0:T(8,128)S(1)}, f32[4,128,128]{1,2,0:T(8,128)S(1)}, u32[]{:S(2)}, u32[]{:S(2)}) collective-permute-start(f32[4,128,128]{1,2,0:T(8,128)S(1)} %reduce_sum.38), channel_id=1, source_target_pairs={{0,1},{1,0},{2,3},{3,2},{4,5},{5,4},{6,7},{7,6},{8,9},{9,8},{10,11... | collective-permute-start | bytes 786440 | tf_op jit(solution)/shard_map/ppermute | solution.py:33
  44.5 8.5 %collective-permute-start.1 = (f32[4,128,128]{1,2,0:T(8,128)S(1)}, f32[4,128,128]{1,2,0:T(8,128)S(1)}, u32[]{:S(2)}, u32[]{:S(2)}) collective-permute-start(f32[4,128,128]{1,2,0:T(8,128)S(1)} %add.98), channel_id=1, source_target_pairs={{0,2},{1,3},{2,0},{3,1},{4,6},{5,7},{6,4},{7,5},{8,10},{9,11},{10,... | collective-permute-start | bytes 786440 | tf_op jit(solution)/shard_map/ppermute | solution.py:33
  53.1 6.5 %collective-permute-start.2 = (f32[4,128,128]{1,2,0:T(8,128)S(1)}, f32[4,128,128]{1,2,0:T(8,128)S(1)}, u32[]{:S(2)}, u32[]{:S(2)}) collective-permute-start(f32[4,128,128]{1,2,0:T(8,128)S(1)} %add.100), channel_id=1, source_target_pairs={{0,4},{1,5},{2,6},{3,7},{4,0},{5,1},{6,2},{7,3},{8,12},{9,13},{10,... | collective-permute-start | bytes 786440 | tf_op jit(solution)/shard_map/ppermute | solution.py:33
  59.6 12.3 %collective-permute-start.3 = (f32[4,128,128]{1,2,0:T(8,128)S(1)}, f32[4,128,128]{1,2,0:T(8,128)S(1)}, u32[]{:S(2)}, u32[]{:S(2)}) collective-permute-start(f32[4,128,128]{1,2,0:T(8,128)S(1)} %add.102), channel_id=1, source_target_pairs={{0,8},{1,9},{2,10},{3,11},{4,12},{5,13},{6,14},{7,15},{8,0},{9,1},... | collective-permute-start | bytes 786440 | tf_op jit(solution)/shard_map/ppermute | solution.py:33
  71.9 17.3 %collective-permute-start.4 = (f32[4,128,128]{1,2,0:T(8,128)S(1)}, f32[4,128,128]{1,2,0:T(8,128)S(1)}, u32[]{:S(2)}, u32[]{:S(2)}) collective-permute-start(f32[4,128,128]{1,2,0:T(8,128)S(1)} %add.104), channel_id=1, source_target_pairs={{0,16},{1,17},{2,18},{3,19},{4,20},{5,21},{6,22},{7,23},{8,24},{9,... | collective-permute-start | bytes 786440 | tf_op jit(solution)/shard_map/ppermute | solution.py:33
where the time goes:
time: 91 us; the launch traced here: 90.7 us
  waiting for transfers between devices  39.2 us (43%)
  starting transfers between devices  19.4 us (21%)
  local copies, waits for them, and re-layouts  18.4 us (20%)
  matrix products  9.51 us (10%)
  other arithmetic  3.88 us (4%)
    ppermute x5, waiting for transfers between devices, from_partner(): lax.ppermute(value, axis, [(i, i ^ 1 << apart) for i in range(lax.axis_si...  33.5 us
    ppermute x5, starting transfers between devices, from_partner(): lax.ppermute(value, axis, [(i, i ^ 1 << apart) for i in range(lax.axis_si...  14.8 us
    gather x3, local copies, waits for them, and re-layouts, local_output(): left_block = (prefix[upper] - prefix[lower]) * active[:, None, None, None]  8.73 us
    all_to_all x1, waiting for transfers between devices, sent_to_all(): return lax.all_to_all(copies, axis, split_axis=0, concat_axis=0, tiled=True)  5.72 us
    all_to_all x1, starting transfers between devices, sent_to_all(): return lax.all_to_all(copies, axis, split_axis=0, concat_axis=0, tiled=True)  4.61 us
    another operation x2, other arithmetic, exclusive_prefix(): return jnp.concatenate([zeros, jnp.cumsum(stacked, axis=0)], axis=0)  3.24 us
    dot_general x2, matrix products, local_output(): jnp.einsum('cthd,chde->cthe', query_blocks, left_block, preferred_element...  3.05 us
    dot_general x1, matrix products, local_output(): jnp.einsum('chts,cshd->cthd', weighted, value_blocks, preferred_element_t...  2.68 us
  transfers between devices with their start and end apart: 6, of which 6 were waited for; matrix products, arithmetic and copies ran while one was open for 28% of the time, Pallas kernels for 0%

commit v1 on v0

v1 whole, which is shorter than its diff:
```python
import jax
import jax.numpy as jnp
from jax import lax
from jax.experimental import pallas as pl
from jax.experimental.pallas import tpu as pltpu
from jax.sharding import PartitionSpec as P

HEADS = 4
HD = 128
SPAN = 128
LEVELS = 16
CLASSES = 16
TOK = 512
SPANS = TOK // SPAN
ROWS = HEADS * HD
PLANE = 32
PLANE_BITS = 5
LAYERS = 8
LAYER_BITS = 3
CH = ROWS // PLANE
EPS = 1e-06
MESH = pl.DeviceIdType.MESH
F32 = jnp.float32
BF16 = jnp.bfloat16


def chunk_row(m):
    return pl.multiple_of(((m % 2) * (PLANE // 2) + m // 2) * CH, CH)


def kernel(
    q_hbm, k_hbm, v_hbm, ids_ref, table_ref, o_ref,
    q, k, v, state, parts, tree, zparts, ztree, left, lam, acc, scaled,
    in_sem, rs_send, rs_recv, lv_send, lv_recv, z_send, z_recv,
):
    outer = lax.axis_index("outer")
    inner = lax.axis_index("inner")
    z = outer // 4
    m = (outer % 4) * 8 + inner

    def plane_dev(mm):
        return {"outer": z * 4 + mm // 8, "inner": mm % 8}

    def layer_dev(zz):
        return {"outer": zz * 4 + outer % 4, "inner": inner}

    loads = [
        pltpu.make_async_copy(src, dst, in_sem.at[n])
        for n, (src, dst) in enumerate(((k_hbm, k), (v_hbm, v), (q_hbm, q)))
    ]
    for c in loads:
        c.start()

    barrier = pltpu.get_barrier_semaphore()

    def greet_plane(j, _):
        pl.semaphore_signal(barrier, inc=1, device_id=plane_dev((m + j) % PLANE), device_id_type=MESH)
        return 0

    def greet_layer(j, _):
        pl.semaphore_signal(barrier, inc=1, device_id=layer_dev((z + j) % LAYERS), device_id_type=MESH)
        return 0

    lax.fori_loop(1, PLANE, greet_plane, 0)
    lax.fori_loop(1, LAYERS, greet_layer, 0)

    def head(h):
        return slice(h * HD, (h + 1) * HD)

    def contract_tokens(a, b):
        return lax.dot_general(a, b, (((0,), (0,)), ((), ())), preferred_element_type=F32)

    loads[0].wait()
    loads[1].wait()
    for h in range(HEADS):
        state[head(h), :] = contract_tokens(k[:, head(h)], v[:, head(h)])

    pl.semaphore_wait(barrier, PLANE - 1 + LAYERS - 1)

    my_row = chunk_row(m)

    def send_chunk(j, _):
        mm = (m + j) % PLANE
        pltpu.make_async_remote_copy(
            src_ref=state.at[pl.ds(chunk_row(mm), CH)],
            dst_ref=parts.at[pl.ds(pl.multiple_of(m * CH, CH), CH)],
            send_sem=rs_send, recv_sem=rs_recv,
            device_id=plane_dev(mm), device_id_type=MESH,
        ).start()
        return 0

    lax.fori_loop(1, PLANE, send_chunk, 0)
    parts[pl.ds(pl.multiple_of(m * CH, CH), CH), :] = state[pl.ds(my_row, CH), :]

    loads[2].wait()
    classes = lax.broadcasted_iota(jnp.int32, (CLASSES, SPAN), 0)
    causal = lax.broadcasted_iota(jnp.int32, (SPAN, SPAN), 0) >= lax.broadcasted_iota(
        jnp.int32, (SPAN, SPAN), 1
    )
    span_rows = [slice(c * SPAN, (c + 1) * SPAN) for c in range(SPANS)]
    for c in range(SPANS):
        hot = (ids_ref[c : c + 1, :] == classes).astype(F32)
        lam[span_rows[c], :] = lax.dot_general(
            hot, table_ref[...], (((0,), (0,)), ((), ())),
            precision=lax.Precision.HIGHEST, preferred_element_type=F32,
        )

    def weight(rows, level, h):
        n = level * HEADS + h
        return lam[rows, n : n + 1]

    for h in range(HEADS):
        spans = [contract_tokens(k[span_rows[c], head(h)], v[span_rows[c], head(h)]) for c in range(3)]
        first = [None, spans[0].astype(BF16), None, spans[2].astype(BF16)]
        second = (spans[0] + spans[1]).astype(BF16)
        for c in range(SPANS):
            rows = span_rows[c]
            q_now = q[rows, head(h)]
            scores = lax.dot_general(
                q_now, k[rows, head(h)], (((1,), (1,)), ((), ())), preferred_element_type=F32
            )
            weighted = jnp.where(causal, scores * weight(rows, 0, h), 0.0).astype(BF16)
            out = jnp.dot(weighted, v[rows, head(h)], preferred_element_type=F32)
            if c % 2 == 1:
                out += weight(rows, 1, h) * jnp.dot(q_now, first[c], preferred_element_type=F32)
            if c >= 2:
                out += weight(rows, 2, h) * jnp.dot(q_now, second, preferred_element_type=F32)
            acc[rows, head(h)] = out

    def plane_wait(send):
        c = pltpu.make_async_remote_copy(
            src_ref=state.at[pl.ds(0, (PLANE - 1) * CH)],
            dst_ref=parts.at[pl.ds(0, (PLANE - 1) * CH)],
            send_sem=rs_send, recv_sem=rs_recv,
            device_id=plane_dev((m + 1) % PLANE), device_id_type=MESH,
        )
        c.wait_send() if send else c.wait_recv()

    plane_wait(False)
    base = [0, 0, 16, 24, 28, 30]
    level = [parts[n * CH : (n + 1) * CH, :] for n in range(PLANE)]
    for b in range(1, PLANE_BITS + 1):
        level = [level[2 * n] + level[2 * n + 1] for n in range(len(level) // 2)]
        for n, value in enumerate(level):
            at = (base[b] + n) * CH
            tree[at : at + CH, :] = value

    total = tree.at[pl.ds(base[PLANE_BITS] * CH, CH)]

    def z_copy(step):
        return pltpu.make_async_remote_copy(
            src_ref=total,
            dst_ref=zparts.at[pl.ds(pl.multiple_of(z * CH, CH), CH)],
            send_sem=z_send.at[step], recv_sem=z_recv.at[step],
            device_id=layer_dev((z + step) % LAYERS), device_id_type=MESH,
        )

    for step in range(1, LAYERS):
        @pl.when(z + step < LAYERS)
        def _(step=step):
            z_copy(step).start()

    def group(b, n):
        src = parts if b == 0 else tree
        return src.at[pl.ds(pl.multiple_of((base[b] + n) * CH, CH), CH)]

    def share(b, src, mm):
        return pltpu.make_async_remote_copy(
            src_ref=src, dst_ref=left.at[b, pl.ds(my_row, CH)],
            send_sem=lv_send.at[b], recv_sem=lv_recv.at[b],
            device_id=plane_dev(mm), device_id_type=MESH,
        )

    for b in range(PLANE_BITS):
        def send_left(n, _, b=b):
            low = n % 2**b
            high = n // 2**b
            mm = high * 2 ** (b + 1) + 2**b + low

            @pl.when(mm != m)
            def _():
                share(b, group(b, 2 * high), mm).start()

            @pl.when(mm == m)
            def _():
                left[b, pl.ds(my_row, CH), :] = group(b, 2 * high)[...]

            return 0

        lax.fori_loop(0, PLANE // 2, send_left, 0)

    bits = [(m // 2**b) % 2 for b in range(PLANE_BITS)] + [(z // 2**b) % 2 for b in range(LAYER_BITS)]

    for b in range(PLANE_BITS + LAYER_BITS):
        @pl.when(bits[b] == 1)
        def _(b=b):
            for h in range(HEADS):
                w = lam[:, (3 + b) * HEADS + h : (3 + b) * HEADS + h + 1]
                scaled[b, :, head(h)] = (q[:, head(h)].astype(F32) * w).astype(BF16)

    for b in range(LAYER_BITS):
        lv = PLANE_BITS + b

        @pl.when(bits[lv] == 1)
        def _(b=b, lv=lv):
            first = (z // 2 ** (b + 1)) * 2 ** (b + 1)
            value = None
            for n in range(2**b):
                zz = first + n
                for step in range(1, LAYERS):
                    @pl.when(z - zz == step)
                    def _(step=step):
                        z_copy(step).wait_recv()
                got = zparts[pl.ds(pl.multiple_of(zz * CH, CH), CH), :]
                value = got if value is None else value + got
            ztree[b] = value
            left[lv, pl.ds(my_row, CH), :] = value

            def send_layer(j, _):
                share(lv, ztree.at[b], (m + j) % PLANE).start()
                return 0

            lax.fori_loop(1, PLANE, send_layer, 0)

    def level_wait(b, count, send):
        c = pltpu.make_async_remote_copy(
            src_ref=left.at[b, pl.ds(0, count * CH)], dst_ref=left.at[b, pl.ds(0, count * CH)],
            send_sem=lv_send.at[b], recv_sem=lv_recv.at[b],
            device_id=plane_dev((m + 1) % PLANE), device_id_type=MESH,
        )
        c.wait_send() if send else c.wait_recv()

    for b in range(PLANE_BITS + LAYER_BITS):
        @pl.when(bits[b] == 1)
        def _(b=b):
            level_wait(b, PLANE - 1, False)
            for h in range(HEADS):
                acc[:, head(h)] += jnp.dot(
                    scaled[b, :, head(h)], left[b, head(h), :].astype(BF16), preferred_element_type=F32
                )

    for h in range(HEADS):
        x = acc[:, head(h)]
        square = jnp.mean(x * x, axis=-1, keepdims=True)
        o_ref[:, head(h)] = (x * lax.rsqrt(square + EPS)).astype(BF16)

    plane_wait(True)
    for step in range(1, LAYERS):
        @pl.when(z + step < LAYERS)
        def _(step=step):
            z_copy(step).wait_send()
    for b in range(PLANE_BITS):
        for bit in range(2):
            @pl.when(bits[b] == bit)
            def _(b=b, bit=bit):
                level_wait(b, PLANE // 2 - bit, True)
    for b in range(PLANE_BITS, PLANE_BITS + LAYER_BITS):
        @pl.when(bits[b] == 1)
        def _(b=b):
            level_wait(b, PLANE - 1, True)


def on_device(query_rows, key_rows, value_rows, level_ids, level_table):
    hbm = pl.BlockSpec(memory_space=pl.ANY)
    vmem = pl.BlockSpec(memory_space=pltpu.VMEM)
    dma = pltpu.SemaphoreType.DMA
    all_levels = PLANE_BITS + LAYER_BITS
    return pl.pallas_call(
        kernel,
        out_shape=jax.ShapeDtypeStruct((TOK, HEADS * HD), BF16),
        in_specs=[hbm, hbm, hbm, vmem, vmem],
        out_specs=vmem,
        scratch_shapes=[
            pltpu.VMEM((TOK, HEADS * HD), BF16),
            pltpu.VMEM((TOK, HEADS * HD), BF16),
            pltpu.VMEM((TOK, HEADS * HD), BF16),
            pltpu.VMEM((ROWS, HD), F32),
            pltpu.VMEM((PLANE * CH, HD), F32),
            pltpu.VMEM((PLANE * CH, HD), F32),
            pltpu.VMEM((LAYERS * CH, HD), F32),
            pltpu.VMEM((LAYER_BITS, CH, HD), F32),
            pltpu.VMEM((all_levels, ROWS, HD), F32),
            pltpu.VMEM((TOK, LEVELS * HEADS), F32),
            pltpu.VMEM((TOK, HEADS * HD), F32),
            pltpu.VMEM((all_levels, TOK, HEADS * HD), BF16),
            dma((3,)), dma, dma, dma((all_levels,)), dma((all_levels,)), dma((LAYERS,)), dma((LAYERS,)),
        ],
        compiler_params=pltpu.CompilerParams(collective_id=0, has_side_effects=True),
        name="fenwick",
    )(
        query_rows, key_rows, value_rows,
        level_ids.reshape(SPANS, SPAN), level_table.reshape(CLASSES, LEVELS * HEADS),
    )


def solution(mesh):
    rows = P(("outer", "inner"), None)
    return jax.shard_map(
        on_device, mesh=mesh,
        in_specs=(rows, rows, rows, P(("outer", "inner")), P()),
        out_specs=rows, check_vma=False,
    )
```

time: 91 us -> 38.9 us (0.43)
  the two profiles are of different devices: /device:TPU:6 before, /device:TPU:255 now
where the time goes in v1:
time: 38.9 us; the launch traced here: 38.7 us
  Pallas kernels  35.3 us (91%)
  local copies, waits for them, and re-layouts  3.38 us (9%)
    pallas_call x1, Pallas kernels, on_device(): pl.pallas_call(kernel, out_shape=jax.ShapeDtypeStruct((TOK, HEADS * HD),...  35.3 us
    unnamed x2, local copies, waits for them, and re-layouts  2.7 us

profile of v1, /device:TPU:255, one launch (start us, length us, event | category | flops | bytes accessed | tf_op | source)
XLA Modules:
  0.0 38.7 jit_solution(868352496818272069)
XLA Ops:
  0.0 0.8 %copy.7 = f32[16,16,4]{0,2,1:T(4,128)S(1)} copy(f32[16,16,4]{1,2,0:T(4,128)} %param.9) | data formatting | bytes 8192 | tf_op args[4]
  0.8 0.7 %copy.8.table_ref = f32[16,64]{1,0:T(8,128)} copy(f32[16,64]{0,1:T(8,128)S(1)} %bitcast.2) | data formatting | bytes 8192 | tf_op jit(solution)/shard_map/reshape | solution.py:292
  1.5 35.3 %fenwick.1 = bf16[512,512]{1,0:T(8,128)(2,1)} custom-call(bf16[512,512]{1,0:T(8,128)(2,1)} %q_hbm.1, bf16[512,512]{1,0:T(8,128)(2,1)} %k_hbm.1, bf16[512,512]{1,0:T(8,128)(2,1)} %v_hbm.1, s32[4,128]{1,0:T(4,128)} %bitcast.3, f32[16,64]{1,0:T(8,128)} %copy.8.table_ref), custom_call_target="tpu_custom_call" | custom-call | tf_op jit(solution)/shard_map/fenwick/pallas_call | solution.py:268
  36.8 1.9 %copy.10 = bf16[512,512]{1,0:T(8,128)(2,1)} copy(bf16[512,512]{1,0:T(8,128)(2,1)} %fenwick.1) | data formatting | bytes 1048576

commit v2 on v1

v2 whole, which is shorter than its diff:
```python
import jax
import jax.numpy as jnp
from jax import lax
from jax.experimental import pallas as pl
from jax.experimental.pallas import tpu as pltpu
from jax.sharding import PartitionSpec as P

HEADS = 4
HD = 128
SPAN = 128
LEVELS = 16
CLASSES = 16
TOK = 512
SPANS = TOK // SPAN
ROWS = HEADS * HD
CHIPS = 16
LAYERS = 8
CHUNKS = 2 * CHIPS
CH = ROWS // CHUNKS
PER_HEAD = CHUNKS // HEADS
EPS = 1e-06
MESH = pl.DeviceIdType.MESH
F32 = jnp.float32
BF16 = jnp.bfloat16

OFFSETS = sorted(
    ((dx, dy) for dx in range(4) for dy in range(4) if dx or dy),
    key=lambda o: -(min(o[0], 4 - o[0]) + min(o[1], 4 - o[1])),
)
STEPS = sorted(range(1, LAYERS), key=lambda s: -min(s, LAYERS - s))


def kernel(
    q_hbm, k_hbm, v_hbm, ids_hbm, table_hbm, o_ref,
    q, k, v, ids, table, state, parts, pack, total, zparts, zsum, zero, low, high, lam, acc, scaled,
    in_sem, rs_send, rs_recv, zero_sem, lo_send, lo_recv, hi_send, hi_recv, fw_send, fw_recv, z_send, z_recv,
):
    outer = lax.axis_index("outer")
    inner = lax.axis_index("inner")
    z, x = lax.div(outer, 4), lax.rem(outer, 4)
    y, c = lax.div(inner, 2), lax.rem(inner, 2)
    p = x * 4 + y
    m = p * 2 + c
    mine = c * CHIPS + p
    xs = [lax.rem(x + dx, 4) for dx in range(4)]
    ys = [lax.rem(y + dy, 4) for dy in range(4)]

    def device(xx, yy, cc):
        return {"outer": z * 4 + xx, "inner": yy * 2 + cc}

    sibling = device(x, y, 1 - c)

    def layer_device(step):
        return {"outer": lax.rem(z + step, LAYERS) * 4 + x, "inner": inner}

    loads = [
        pltpu.make_async_copy(src, dst, in_sem.at[n])
        for n, (src, dst) in enumerate(
            ((k_hbm, k), (v_hbm, v), (ids_hbm, ids), (table_hbm, table), (q_hbm, q))
        )
    ]
    for load in loads:
        load.start()

    barrier = pltpu.get_barrier_semaphore()

    def greet(dev):
        pl.semaphore_signal(barrier, inc=1, device_id=dev, device_id_type=MESH)

    for dx, dy in OFFSETS:
        for cc in range(2):
            greet(device(xs[dx], ys[dy], cc))
    for step in STEPS:
        greet(layer_device(step))
    greet(sibling)

    def head(h):
        return slice(h * HD, (h + 1) * HD)

    def head_chunks(h):
        return slice(h * PER_HEAD, (h + 1) * PER_HEAD)

    def contract_tokens(a, b):
        return lax.dot_general(a, b, (((0,), (0,)), ((), ())), preferred_element_type=F32)

    loads[0].wait()
    loads[1].wait()
    for h in range(HEADS):
        state[head_chunks(h)] = contract_tokens(k[:, head(h)], v[:, head(h)]).reshape(PER_HEAD, CH, HD)

    pl.semaphore_wait(barrier, CHUNKS - 1 + LAYERS - 1)

    def to_owner(xx, yy, cc):
        return pltpu.make_async_remote_copy(
            src_ref=state.at[cc * CHIPS + xx * 4 + yy], dst_ref=parts.at[m],
            send_sem=rs_send, recv_sem=rs_recv,
            device_id=device(xx, yy, cc), device_id_type=MESH,
        )

    for dx, dy in OFFSETS:
        for cc in range(2):
            to_owner(xs[dx], ys[dy], cc).start()
    to_owner(x, y, 1 - c).start()
    parts[m] = state[mine]

    def zero_copy():
        return pltpu.make_async_remote_copy(
            src_ref=state, dst_ref=zero, send_sem=zero_sem.at[0], recv_sem=zero_sem.at[1],
            device_id=sibling, device_id_type=MESH,
        )

    @pl.when(c == 0)
    def _():
        zero_copy().start()

    bits = (
        [c]
        + [lax.rem(lax.div(p, 2**b), 2) for b in range(4)]
        + [lax.rem(lax.div(z, 2**b), 2) for b in range(3)]
    )
    for load in loads[2:]:
        load.wait()
    classes = lax.broadcasted_iota(jnp.int32, (CLASSES, SPAN), 0)
    causal = lax.broadcasted_iota(jnp.int32, (SPAN, SPAN), 0) >= lax.broadcasted_iota(
        jnp.int32, (SPAN, SPAN), 1
    )
    span_rows = [slice(n * SPAN, (n + 1) * SPAN) for n in range(SPANS)]
    for n in range(SPANS):
        hot = (ids[n : n + 1, :] == classes).astype(F32)
        for h in range(HEADS):
            lam[span_rows[n], h * LEVELS : (h + 1) * LEVELS] = lax.dot_general(
                hot, table[:, h, :], (((0,), (0,)), ((), ())),
                precision=lax.Precision.HIGHEST, preferred_element_type=F32,
            )

    def weight(rows, level, h):
        n = h * LEVELS + level
        return lam[rows, n : n + 1]

    for h in range(HEADS):
        spans = [contract_tokens(k[span_rows[n], head(h)], v[span_rows[n], head(h)]) for n in range(3)]
        first = [None, spans[0].astype(BF16), None, spans[2].astype(BF16)]
        second = (spans[0] + spans[1]).astype(BF16)
        for n in range(SPANS):
            rows = span_rows[n]
            q_now = q[rows, head(h)]
            scores = lax.dot_general(
                q_now, k[rows, head(h)], (((1,), (1,)), ((), ())), preferred_element_type=F32
            )
            weighted = jnp.where(causal, scores * weight(rows, 0, h), 0.0).astype(BF16)
            out = jnp.dot(weighted, v[rows, head(h)], preferred_element_type=F32)
            if n % 2 == 1:
                out += weight(rows, 1, h) * jnp.dot(q_now, first[n], preferred_element_type=F32)
            if n >= 2:
                out += weight(rows, 2, h) * jnp.dot(q_now, second, preferred_element_type=F32)
            acc[rows, head(h)] = out

    def scale(b):
        @pl.when(bits[b] == 1)
        def _():
            for h in range(HEADS):
                scaled[b, :, head(h)] = (q[:, head(h)].astype(F32) * weight(slice(0, TOK), 3 + b, h)).astype(BF16)

    for b in range(SCALE_FIRST):
        scale(b)

    def bytes_of(n, send_sem, recv_sem):
        return pltpu.make_async_remote_copy(
            src_ref=parts.at[pl.ds(0, n)], dst_ref=parts.at[pl.ds(0, n)],
            send_sem=send_sem, recv_sem=recv_sem, device_id=sibling, device_id_type=MESH,
        )

    bytes_of(CHUNKS - 1, rs_send, rs_recv).wait_recv()
    groups = [[parts[n] for n in range(CHUNKS)]]
    for b in range(5):
        below = groups[-1]
        groups.append([below[2 * n] + below[2 * n + 1] for n in range(len(below) // 2)])
    total[...] = groups[5][0]

    def z_copy(step):
        return pltpu.make_async_remote_copy(
            src_ref=total, dst_ref=zparts.at[z],
            send_sem=z_send.at[step], recv_sem=z_recv.at[step],
            device_id=layer_device(step), device_id_type=MESH,
        )

    for step in STEPS:
        @pl.when(z + step < LAYERS)
        def _(step=step):
            z_copy(step).start()

    for chip in range(1, CHIPS):
        ones = [b for b in range(4) if chip >> b & 1]
        for slot, b in enumerate(ones):
            pack[chip, slot] = groups[b + 1][(chip >> b) - 1]
    count = bits[1] + bits[2] + bits[3] + bits[4]

    for dx, dy in OFFSETS:
        xx, yy = xs[dx], ys[dy]
        chip = xx * 4 + yy
        ones = lax.rem(xx, 2) + lax.div(xx, 2) + lax.rem(yy, 2) + lax.div(yy, 2)
        for n in range(1, 5):
            @pl.when(ones == n)
            def _(xx=xx, yy=yy, chip=chip, n=n):
                pltpu.make_async_remote_copy(
                    src_ref=pack.at[chip, pl.ds(0, n)], dst_ref=low.at[pl.ds(0, n), mine],
                    send_sem=lo_send, recv_sem=lo_recv,
                    device_id=device(xx, yy, c), device_id_type=MESH,
                ).start()
    for slot in range(4):
        @pl.when(slot < count)
        def _(slot=slot):
            low[slot, mine] = pack[p, slot]

    for b in range(SCALE_FIRST, 8):
        scale(b)

    def share(b, xx, yy, cc):
        return pltpu.make_async_remote_copy(
            src_ref=zsum.at[b], dst_ref=high.at[b, mine],
            send_sem=hi_send.at[b], recv_sem=hi_recv.at[b],
            device_id=device(xx, yy, cc), device_id_type=MESH,
        )

    direct = [False, False, LAST_DIRECT]
    for b in range(3):
        @pl.when(bits[5 + b] == 1)
        def _(b=b):
            first = lax.div(z, 2 ** (b + 1)) * 2 ** (b + 1)
            value = None
            for n in range(2**b):
                for step in range(1, LAYERS):
                    @pl.when(z - (first + n) == step)
                    def _(step=step):
                        z_copy(step).wait_recv()
                got = zparts[first + n]
                value = got if value is None else value + got
            zsum[b] = value
            for dx, dy in OFFSETS:
                share(b, xs[dx], ys[dy], c).start()
                if direct[b]:
                    share(b, xs[dx], ys[dy], 1 - c).start()
            if direct[b]:
                share(b, x, y, 1 - c).start()
            high[b, mine] = value

    half = pl.ds(c * CHIPS, CHIPS)

    def low_forward(n):
        return pltpu.make_async_remote_copy(
            src_ref=low.at[pl.ds(0, n), half], dst_ref=low.at[pl.ds(0, n), half],
            send_sem=fw_send.at[0], recv_sem=fw_recv.at[0], device_id=sibling, device_id_type=MESH,
        )

    def high_forward(b):
        return pltpu.make_async_remote_copy(
            src_ref=high.at[b, half], dst_ref=high.at[b, half],
            send_sem=fw_send.at[1 + b], recv_sem=fw_recv.at[1 + b], device_id=sibling, device_id_type=MESH,
        )

    def low_wait(n, send):
        copy = pltpu.make_async_remote_copy(
            src_ref=low.at[pl.ds(0, n), pl.ds(0, CHIPS - 1)], dst_ref=low.at[pl.ds(0, n), pl.ds(0, CHIPS - 1)],
            send_sem=lo_send, recv_sem=lo_recv, device_id=sibling, device_id_type=MESH,
        )
        copy.wait_send() if send else copy.wait_recv()

    def add(b, matrices):
        for h in range(HEADS):
            acc[:, head(h)] += jnp.dot(
                scaled[b, :, head(h)],
                matrices[head_chunks(h)].reshape(HD, HD).astype(BF16),
                preferred_element_type=F32,
            )

    for n in range(1, 5):
        @pl.when(count == n)
        def _(n=n):
            low_wait(n, False)
            low_forward(n).start()

    @pl.when(c == 1)
    def _():
        zero_copy().wait_recv()
        add(0, zero)

    for b in range(3):
        if not direct[b]:
            @pl.when(bits[5 + b] == 1)
            def _(b=b):
                bytes_of(CHIPS - 1, hi_send.at[b], hi_recv.at[b]).wait_recv()
                high_forward(b).start()

    for n in range(1, 5):
        @pl.when(count == n)
        def _(n=n):
            low_forward(n).wait_recv()
    slot = 0
    for b in range(1, 5):
        @pl.when(bits[b] == 1)
        def _(b=b, slot=slot):
            add(b, low.at[slot])
        slot = slot + bits[b]

    for b in range(3):
        @pl.when(bits[5 + b] == 1)
        def _(b=b):
            if direct[b]:
                bytes_of(CHUNKS - 1, hi_send.at[b], hi_recv.at[b]).wait_recv()
            else:
                high_forward(b).wait_recv()
            add(5 + b, high.at[b])

    for h in range(HEADS):
        value = acc[:, head(h)]
        square = jnp.mean(value * value, axis=-1, keepdims=True)
        o_ref[:, head(h)] = (value * lax.rsqrt(square + EPS)).astype(BF16)

    bytes_of(CHUNKS - 1, rs_send, rs_recv).wait_send()

    @pl.when(c == 0)
    def _():
        zero_copy().wait_send()

    for step in STEPS:
        @pl.when(z + step < LAYERS)
        def _(step=step):
            z_copy(step).wait_send()
    for n in range(5):
        @pl.when(count == n)
        def _(n=n):
            bytes_of(CHUNKS - n, lo_send, lo_recv).wait_send()
            if n:
                low_forward(n).wait_send()
    for b in range(3):
        @pl.when(bits[5 + b] == 1)
        def _(b=b):
            if direct[b]:
                bytes_of(CHUNKS - 1, hi_send.at[b], hi_recv.at[b]).wait_send()
            else:
                bytes_of(CHIPS - 1, hi_send.at[b], hi_recv.at[b]).wait_send()
                high_forward(b).wait_send()


SCALE_FIRST = 4
LAST_DIRECT = False


def on_device(query_rows, key_rows, value_rows, level_ids, level_table):
    hbm = pl.BlockSpec(memory_space=pl.ANY)
    vmem = pl.BlockSpec(memory_space=pltpu.VMEM)
    dma = pltpu.SemaphoreType.DMA
    wide = (TOK, HEADS * HD)
    return pl.pallas_call(
        kernel,
        out_shape=jax.ShapeDtypeStruct(wide, BF16),
        in_specs=[hbm] * 5,
        out_specs=vmem,
        scratch_shapes=[
            pltpu.VMEM(wide, BF16),
            pltpu.VMEM(wide, BF16),
            pltpu.VMEM(wide, BF16),
            pltpu.VMEM((SPANS, SPAN), jnp.int32),
            pltpu.VMEM((CLASSES, HEADS, LEVELS), F32),
            pltpu.VMEM((CHUNKS, CH, HD), F32),
            pltpu.VMEM((CHUNKS, CH, HD), F32),
            pltpu.VMEM((CHIPS, 4, CH, HD), F32),
            pltpu.VMEM((CH, HD), F32),
            pltpu.VMEM((LAYERS, CH, HD), F32),
            pltpu.VMEM((3, CH, HD), F32),
            pltpu.VMEM((CHUNKS, CH, HD), F32),
            pltpu.VMEM((4, CHUNKS, CH, HD), F32),
            pltpu.VMEM((3, CHUNKS, CH, HD), F32),
            pltpu.VMEM((TOK, LEVELS * HEADS), F32),
            pltpu.VMEM(wide, F32),
            pltpu.VMEM((8, *wide), BF16),
            dma((5,)), dma, dma, dma((2,)), dma, dma, dma((3,)), dma((3,)), dma((4,)), dma((4,)),
            dma((LAYERS,)), dma((LAYERS,)),
        ],
        compiler_params=pltpu.CompilerParams(collective_id=0, has_side_effects=True),
        name="fenwick",
    )(
        query_rows, key_rows, value_rows,
        level_ids.reshape(SPANS, SPAN), jnp.transpose(level_table, (0, 2, 1)),
    )


def solution(mesh):
    rows = P(("outer", "inner"), None)
    return jax.shard_map(
        on_device, mesh=mesh,
        in_specs=(rows, rows, rows, P(("outer", "inner")), P()),
        out_specs=rows, check_vma=False,
    )
```

time: 38.9 us -> 28.5 us (0.73)
  Pallas kernels: 35.3 us -> 26.4 us
  local copies, waits for them, and re-layouts: 3.38 us -> 1.87 us
    pallas_call x1, Pallas kernels: 35.3 us -> 26.4 us  [on_device(): pl.pallas_call(kernel, out_shape=jax.ShapeDtypeStruct(wide, BF16), in_spe...]
    unnamed x2 -> x1, local copies, waits for them, and re-layouts: 2.7 us -> 1.87 us
    reshape x1 -> x0, local copies, waits for them, and re-layouts: 0.67 us -> none  [on_device(): level_table.reshape(CLASSES, LEVELS * HEADS)]
where the time goes in v2:
time: 28.5 us; the launch traced here: 28.3 us
  Pallas kernels  26.4 us (93%)
  local copies, waits for them, and re-layouts  1.87 us (7%)
    pallas_call x1, Pallas kernels, on_device(): pl.pallas_call(kernel, out_shape=jax.ShapeDtypeStruct(wide, BF16), in_spe...  26.4 us
    unnamed x1, local copies, waits for them, and re-layouts  1.87 us

profile of v2, /device:TPU:255, one launch (start us, length us, event | category | flops | bytes accessed | tf_op | source)
XLA Modules:
  0.0 28.3 jit_solution(15294240003637677747)
XLA Ops:
  0.0 26.4 %fenwick.1 = bf16[512,512]{1,0:T(8,128)(2,1)} custom-call(bf16[512,512]{1,0:T(8,128)(2,1)} %q_hbm.1, bf16[512,512]{1,0:T(8,128)(2,1)} %k_hbm.1, bf16[512,512]{1,0:T(8,128)(2,1)} %v_hbm.1, s32[4,128]{1,0:T(4,128)} %bitcast.3, f32[16,4,16]{2,1,0:T(4,128)} %bitcast.2), custom_call_target="tpu_custom_call" | custom-call | tf_op jit(solution)/shard_map/fenwick/pallas_call | solution.py:354
  26.4 1.9 %copy.7 = bf16[512,512]{1,0:T(8,128)(2,1)} copy(bf16[512,512]{1,0:T(8,128)(2,1)} %fenwick.1) | data formatting | bytes 1048576

commit v3 on v2

--- a/solution.py
+++ b/solution.py
@@ -31,9 +31,9 @@
 
 
 def kernel(
-    q_hbm, k_hbm, v_hbm, ids_hbm, table_hbm, o_ref,
-    q, k, v, ids, table, state, parts, pack, total, zparts, zsum, zero, low, high, lam, acc, scaled,
-    in_sem, rs_send, rs_recv, zero_sem, lo_send, lo_recv, hi_send, hi_recv, fw_send, fw_recv, z_send, z_recv,
+    q_hbm, k_hbm, v_hbm, ids_hbm, table_hbm, acc,
+    q, k, v, ids, table, state, parts, pack, total, zparts, zsum, zero, low, high, lam, scaled,
+    in_sem, rs_send, rs_recv, zero_sem, lo_send, lo_recv, hi_send, hi_recv, fw_send, fw_recv, z_send, z_recv, ready,
 ):
     outer = lax.axis_index("outer")
     inner = lax.axis_index("inner")
@@ -70,9 +70,11 @@
     for dx, dy in OFFSETS:
         for cc in range(2):
             greet(device(xs[dx], ys[dy], cc))
+    greet(sibling)
     for step in STEPS:
-        greet(layer_device(step))
-    greet(sibling)
+        @pl.when(z + step < LAYERS)
+        def _(step=step):
+            greet(layer_device(step))
 
     def head(h):
         return slice(h * HD, (h + 1) * HD)
@@ -88,7 +90,7 @@
     for h in range(HEADS):
         state[head_chunks(h)] = contract_tokens(k[:, head(h)], v[:, head(h)]).reshape(PER_HEAD, CH, HD)
 
-    pl.semaphore_wait(barrier, CHUNKS - 1 + LAYERS - 1)
+    pl.semaphore_wait(barrier, CHUNKS - 1 + z)
 
     def to_owner(xx, yy, cc):
         return pltpu.make_async_remote_copy(
@@ -102,6 +104,14 @@
             to_owner(xs[dx], ys[dy], cc).start()
     to_owner(x, y, 1 - c).start()
     parts[m] = state[mine]
+
+    def below(step):
+        return {"outer": lax.rem(z + LAYERS - step, LAYERS) * 4 + x, "inner": inner}
+
+    for step in STEPS:
+        @pl.when(step <= z)
+        def _(step=step):
+            pl.semaphore_signal(ready.at[step], inc=1, device_id=below(step), device_id_type=MESH)
 
     def zero_copy():
         return pltpu.make_async_remote_copy(
@@ -187,6 +197,7 @@
     for step in STEPS:
         @pl.when(z + step < LAYERS)
         def _(step=step):
+            pl.semaphore_wait(ready.at[step], 1)
             z_copy(step).start()
 
     for chip in range(1, CHIPS):
@@ -223,7 +234,7 @@
         )
 
     direct = [False, False, LAST_DIRECT]
-    for b in range(3):
+    for b in HIGH_ORDER:
         @pl.when(bits[5 + b] == 1)
         def _(b=b):
             first = lax.div(z, 2 ** (b + 1)) * 2 ** (b + 1)
@@ -311,11 +322,6 @@
                 high_forward(b).wait_recv()
             add(5 + b, high.at[b])
 
-    for h in range(HEADS):
-        value = acc[:, head(h)]
-        square = jnp.mean(value * value, axis=-1, keepdims=True)
-        o_ref[:, head(h)] = (value * lax.rsqrt(square + EPS)).astype(BF16)
-
     bytes_of(CHUNKS - 1, rs_send, rs_recv).wait_send()
 
     @pl.when(c == 0)
@@ -343,17 +349,26 @@
 
 
 SCALE_FIRST = 4
+HIGH_ORDER = (2, 0, 1)
 LAST_DIRECT = False
 
 
+def normalize(x_ref, o_ref):
+    for h in range(HEADS):
+        cols = slice(h * HD, (h + 1) * HD)
+        value = x_ref[:, cols]
+        square = jnp.mean(value * value, axis=-1, keepdims=True)
+        o_ref[:, cols] = (value * lax.rsqrt(square + EPS)).astype(BF16)
+
+
 def on_device(query_rows, key_rows, value_rows, level_ids, level_table):
-    hbm = pl.BlockSpec(memory_space=pl.ANY)
+    hbm = pl.BlockSpec(memory_space=pltpu.HBM)
     vmem = pl.BlockSpec(memory_space=pltpu.VMEM)
     dma = pltpu.SemaphoreType.DMA
     wide = (TOK, HEADS * HD)
-    return pl.pallas_call(
+    unnormed = pl.pallas_call(
         kernel,
-        out_shape=jax.ShapeDtypeStruct(wide, BF16),
+        out_shape=jax.ShapeDtypeStruct(wide, F32),
         in_specs=[hbm] * 5,
         out_specs=vmem,
         scratch_shapes=[
@@ -372,17 +387,29 @@
             pltpu.VMEM((4, CHUNKS, CH, HD), F32),
             pltpu.VMEM((3, CHUNKS, CH, HD), F32),
             pltpu.VMEM((TOK, LEVELS * HEADS), F32),
-            pltpu.VMEM(wide, F32),
             pltpu.VMEM((8, *wide), BF16),
             dma((5,)), dma, dma, dma((2,)), dma, dma, dma((3,)), dma((3,)), dma((4,)), dma((4,)),
-            dma((LAYERS,)), dma((LAYERS,)),
+            dma((LAYERS,)), dma((LAYERS,)), pltpu.SemaphoreType.REGULAR((LAYERS,)),
         ],
-        compiler_params=pltpu.CompilerParams(collective_id=0, has_side_effects=True),
+        compiler_params=pltpu.CompilerParams(collective_id=0, has_side_effects=True, vmem_limit_bytes=24 * 2**20),
         name="fenwick",
     )(
-        query_rows, key_rows, value_rows,
-        level_ids.reshape(SPANS, SPAN), jnp.transpose(level_table, (0, 2, 1)),
+        *[
+            pltpu.with_memory_space_constraint(a, pltpu.HBM)
+            for a in (
+                query_rows, key_rows, value_rows,
+                level_ids.reshape(SPANS, SPAN), jnp.transpose(level_table, (0, 2, 1)),
+            )
+        ]
     )
+    return pl.pallas_call(
+        normalize,
+        out_shape=jax.ShapeDtypeStruct(wide, BF16),
+        in_specs=[vmem],
+        out_specs=vmem,
+        compiler_params=pltpu.CompilerParams(vmem_limit_bytes=8 * 2**20),
+        name="normalize",
+    )(unnormed)
 
 
 def solution(mesh):

time: 28.5 us -> 26.6 us (0.933)
  local copies, waits for them, and re-layouts: 1.87 us -> 0 us
    unnamed x1 -> x0, local copies, waits for them, and re-layouts: 1.87 us -> none
    pallas_call x1 -> x2, Pallas kernels: 26.4 us -> 26.5 us  [the longest x1 25.3 us: on_device(): pl.pallas_call(kernel, out_shape=jax.ShapeDtypeStruct(wide, F32), in_spec...]
where the time goes in v3:
time: 26.6 us; the launch traced here: 26.5 us
  Pallas kernels  26.5 us (100%)
    pallas_call x1, Pallas kernels, on_device(): pl.pallas_call(kernel, out_shape=jax.ShapeDtypeStruct(wide, F32), in_spec...  25.3 us
    pallas_call x1, Pallas kernels, on_device(): pl.pallas_call(normalize, out_shape=jax.ShapeDtypeStruct(wide, BF16), in_...  1.15 us

profile of v3, /device:TPU:255, one launch (start us, length us, event | category | flops | bytes accessed | tf_op | source)
XLA Modules:
  0.0 26.5 jit_solution(10247349658047896503)
XLA Ops:
  0.0 25.3 %fenwick.1.x_ref = f32[512,512]{1,0:T(8,128)S(1)} custom-call(bf16[512,512]{1,0:T(8,128)(2,1)} %q_hbm.1, bf16[512,512]{1,0:T(8,128)(2,1)} %k_hbm.1, bf16[512,512]{1,0:T(8,128)(2,1)} %v_hbm.1, s32[4,128]{1,0:T(4,128)} %bitcast.3, f32[16,4,16]{2,1,0:T(4,128)} %bitcast.2), custom_call_target="tpu_custom_call" | custom-call | tf_op jit(solution)/shard_map/fenwick/pallas_call | solution.py:369
  25.3 1.1 %normalize.1 = bf16[512,512]{1,0:T(8,128)(2,1)} custom-call(f32[512,512]{1,0:T(8,128)S(1)} %fenwick.1.x_ref), custom_call_target="tpu_custom_call" | custom-call | tf_op jit(solution)/shard_map/normalize/pallas_call | solution.py:405

commit v4 on v3

v4 whole, which is shorter than its diff:
```python
import jax
import jax.numpy as jnp
from jax import lax
from jax.experimental import pallas as pl
from jax.experimental.pallas import tpu as pltpu
from jax.sharding import PartitionSpec as P

HEADS = 4
HD = 128
SPAN = 128
LEVELS = 16
CLASSES = 16
TOK = 512
SPANS = TOK // SPAN
CHIPS = 16
LAYERS = 8
CHUNKS = 2 * CHIPS
CH = HEADS * HD // CHUNKS
PER_HEAD = CHUNKS // HEADS
HALF = HEADS * HD // 2
EPS = 1e-06
MESH = pl.DeviceIdType.MESH
F32 = jnp.float32
BF16 = jnp.bfloat16

OFFSETS = sorted(
    ((dx, dy) for dx in range(4) for dy in range(4) if dx or dy),
    key=lambda o: -(min(o[0], 4 - o[0]) + min(o[1], 4 - o[1])),
)
STEPS = sorted(range(1, LAYERS), key=lambda s: -min(s, LAYERS - s))
SCALE_FIRST = 4
HIGH_ORDER = (0, 2, 1)
Y_EARLY = True


def kernel(
    q_hbm, k_hbm, v_hbm, ids_hbm, table_hbm, acc,
    q, k, v, ids, table, state, other, chip_state, parts, sums, total, five, six, zparts, zsum, zero, pair, low, high,
    lam, scaled,
    in_sem, other_sem, rs_send, rs_recv, zero_sem, y_send, y_recv, lo_send, lo_recv, hi_send, hi_recv, fw_send, fw_recv,
    z_send, z_recv, five_send, five_recv, six_send, six_recv, ready,
):
    outer = lax.axis_index("outer")
    inner = lax.axis_index("inner")
    z, x = lax.div(outer, 4), lax.rem(outer, 4)
    y, c = lax.div(inner, 2), lax.rem(inner, 2)
    p = x * 4 + y
    place = lax.rem(z, 4)
    mine = c * CHIPS + p
    xs = [lax.rem(x + dx, 4) for dx in range(4)]
    ys = [lax.rem(y + dy, 4) for dy in range(4)]

    def device(xx, yy, cc, layer=None):
        return {"outer": (z if layer is None else layer) * 4 + xx, "inner": yy * 2 + cc}

    sibling = device(x, y, 1 - c)

    def in_layer(layer):
        return {"outer": layer * 4 + x, "inner": inner}

    def columns(cc):
        return pl.ds(pl.multiple_of(cc * HALF, HALF), HALF)

    def load(src, dst, n):
        return pltpu.make_async_copy(src, dst, in_sem.at[n])

    key_loads = [
        [
            load(src.at[:, columns(cc)], dst.at[:, columns(cc)], 2 * n + i)
            for i, (src, dst) in enumerate(((k_hbm, k), (v_hbm, v)))
        ]
        for n, cc in enumerate((1 - c, c))
    ]
    late_loads = [load(ids_hbm, ids, 4), load(table_hbm, table, 5), load(q_hbm, q, 6)]
    for copy in key_loads[0] + key_loads[1] + late_loads:
        copy.start()

    barrier = pltpu.get_barrier_semaphore()

    def greet(dev):
        pl.semaphore_signal(barrier, inc=1, device_id=dev, device_id_type=MESH)

    for dx, dy in OFFSETS:
        greet(device(xs[dx], ys[dy], c))
    greet(sibling)
    for step in STEPS:
        @pl.when(z + step < LAYERS)
        def _(step=step):
            greet(in_layer(z + step))

    def head(h):
        return slice(h * HD, (h + 1) * HD)

    def head_chunks(h):
        return slice(h * PER_HEAD, (h + 1) * PER_HEAD)

    def contract_tokens(a, b):
        return lax.dot_general(a, b, (((0,), (0,)), ((), ())), preferred_element_type=F32)

    def half_state(n, cc):
        for copy in key_loads[n]:
            copy.wait()
        for i in range(HEADS // 2):
            cols = pl.ds(pl.multiple_of(cc * HALF + i * HD, HD), HD)
            value = contract_tokens(k[:, cols], v[:, cols])
            state[pl.ds(cc * CHIPS + i * PER_HEAD, PER_HEAD)] = value.reshape(PER_HEAD, CH, HD)

    half_state(0, 1 - c)
    pl.semaphore_wait(barrier, CHIPS - 1 + 1 + z)
    half, other_half = pl.ds(c * CHIPS, CHIPS), pl.ds((1 - c) * CHIPS, CHIPS)
    other_copy = pltpu.make_async_remote_copy(
        src_ref=state.at[other_half], dst_ref=other,
        send_sem=other_sem.at[0], recv_sem=other_sem.at[1], device_id=sibling, device_id_type=MESH,
    )
    other_copy.start()
    half_state(1, c)

    for step in STEPS:
        @pl.when(step <= z)
        def _(step=step):
            pl.semaphore_signal(ready.at[step], inc=1, device_id=in_layer(z - step), device_id_type=MESH)

    other_copy.wait_recv()
    chip_state[...] = state[half] + other[...]

    def to_owner(xx, yy):
        return pltpu.make_async_remote_copy(
            src_ref=chip_state.at[xx * 4 + yy], dst_ref=parts.at[p],
            send_sem=rs_send, recv_sem=rs_recv,
            device_id=device(xx, yy, c), device_id_type=MESH,
        )

    for dx, dy in OFFSETS:
        to_owner(xs[dx], ys[dy]).start()
    parts[p] = chip_state[p]

    straight = ((0, 3, 1), (1, 3, 2), (0, 2, 1), (1, 2, 2), (0, 1, 0), (2, 3, 0))

    def straight_copy(to, slot):
        dst = low.at[0, half] if slot == 0 else pair.at[slot - 1]
        return pltpu.make_async_remote_copy(
            src_ref=chip_state, dst_ref=dst,
            send_sem=y_send.at[to], recv_sem=y_recv.at[slot],
            device_id=device(x, to, c), device_id_type=MESH,
        )

    def start_straight():
        for at, to, slot in straight:
            @pl.when(y == at)
            def _(to=to, slot=slot):
                straight_copy(to, slot).start()

    if Y_EARLY:
        start_straight()

    zero_copy = pltpu.make_async_remote_copy(
        src_ref=state.at[pl.ds(0, CHIPS)], dst_ref=zero, send_sem=zero_sem.at[0], recv_sem=zero_sem.at[1],
        device_id=sibling, device_id_type=MESH,
    )

    @pl.when(c == 0)
    def _():
        zero_copy.start()

    bits = (
        [c]
        + [lax.rem(lax.div(p, 2**b), 2) for b in range(4)]
        + [lax.rem(lax.div(z, 2**b), 2) for b in range(3)]
    )
    for copy in late_loads:
        copy.wait()
    classes = lax.broadcasted_iota(jnp.int32, (CLASSES, SPAN), 0)
    causal = lax.broadcasted_iota(jnp.int32, (SPAN, SPAN), 0) >= lax.broadcasted_iota(
        jnp.int32, (SPAN, SPAN), 1
    )
    span_rows = [slice(n * SPAN, (n + 1) * SPAN) for n in range(SPANS)]
    for n in range(SPANS):
        hot = (ids[n : n + 1, :] == classes).astype(F32)
        for h in range(HEADS):
            lam[span_rows[n], h * LEVELS : (h + 1) * LEVELS] = lax.dot_general(
                hot, table[:, h, :], (((0,), (0,)), ((), ())),
                precision=lax.Precision.HIGHEST, preferred_element_type=F32,
            )

    def weight(rows, level, h):
        n = h * LEVELS + level
        return lam[rows, n : n + 1]

    for h in range(HEADS):
        spans = [contract_tokens(k[span_rows[n], head(h)], v[span_rows[n], head(h)]) for n in range(3)]
        first = [None, spans[0].astype(BF16), None, spans[2].astype(BF16)]
        second = (spans[0] + spans[1]).astype(BF16)
        for n in range(SPANS):
            rows = span_rows[n]
            q_now = q[rows, head(h)]
            scores = lax.dot_general(
                q_now, k[rows, head(h)], (((1,), (1,)), ((), ())), preferred_element_type=F32
            )
            weighted = jnp.where(causal, scores * weight(rows, 0, h), 0.0).astype(BF16)
            out = jnp.dot(weighted, v[rows, head(h)], preferred_element_type=F32)
            if n % 2 == 1:
                out += weight(rows, 1, h) * jnp.dot(q_now, first[n], preferred_element_type=F32)
            if n >= 2:
                out += weight(rows, 2, h) * jnp.dot(q_now, second, preferred_element_type=F32)
            acc[rows, head(h)] = out

    def scale(b):
        @pl.when(bits[b] == 1)
        def _():
            for h in range(HEADS):
                scaled[b, :, head(h)] = (q[:, head(h)].astype(F32) * weight(slice(0, TOK), 3 + b, h)).astype(BF16)

    for b in range(SCALE_FIRST):
        scale(b)

    def bytes_of(n, send_sem, recv_sem):
        return pltpu.make_async_remote_copy(
            src_ref=state.at[pl.ds(0, n)], dst_ref=state.at[pl.ds(0, n)],
            send_sem=send_sem, recv_sem=recv_sem, device_id=sibling, device_id_type=MESH,
        )

    bytes_of(CHIPS - 1, rs_send, rs_recv).wait_recv()
    groups = [[parts[n] for n in range(CHIPS)]]
    for b in range(4):
        below = groups[-1]
        groups.append([below[2 * n] + below[2 * n + 1] for n in range(len(below) // 2)])
    total[...] = groups[4][0]

    def six_copy(step):
        return pltpu.make_async_remote_copy(
            src_ref=total, dst_ref=six.at[place],
            send_sem=six_send.at[step - 1], recv_sem=six_recv.at[place],
            device_id=in_layer(z + step), device_id_type=MESH,
        )

    six_steps = [(3, 2), (2, 1)]
    for at, steps in enumerate(six_steps):
        @pl.when(place == at)
        def _(steps=steps):
            for step in steps:
                pl.semaphore_wait(ready.at[step], 1)
                six_copy(step).start()

    five_copy = pltpu.make_async_remote_copy(
        src_ref=total, dst_ref=five.at[0],
        send_sem=five_send, recv_sem=five_recv.at[0],
        device_id=in_layer(z + 1), device_id_type=MESH,
    )

    @pl.when(bits[5] == 0)
    def _():
        pl.semaphore_wait(ready.at[1], 1)
        five_copy.start()

    sums[0], sums[1], sums[2] = groups[2][0], groups[2][2], groups[3][0]

    def low_copy(level, xx, yy):
        src = sums.at[lax.div(xx, 2)] if level == 3 else sums.at[2]
        return pltpu.make_async_remote_copy(
            src_ref=src, dst_ref=low.at[level - 1, mine],
            send_sem=lo_send.at[level - 3], recv_sem=lo_recv.at[level - 3],
            device_id=device(xx, yy, c), device_id_type=MESH,
        )

    for dx, dy in OFFSETS:
        xx, yy = xs[dx], ys[dy]
        for level, bit in ((3, lax.rem(xx, 2)), (4, lax.div(xx, 2))):
            @pl.when(bit == 1)
            def _(level=level, xx=xx, yy=yy):
                low_copy(level, xx, yy).start()
    low[2, mine] = sums[lax.div(x, 2)]
    low[3, mine] = sums[2]

    if not Y_EARLY:
        start_straight()

    def z_copy(layer):
        return pltpu.make_async_remote_copy(
            src_ref=total, dst_ref=zparts.at[z],
            send_sem=z_send.at[layer - 4], recv_sem=z_recv.at[z],
            device_id=in_layer(layer), device_id_type=MESH,
        )

    @pl.when(z < 4)
    def _():
        for layer in (7, 6, 5, 4):
            pl.semaphore_wait(ready.at[layer - z], 1)
            z_copy(layer).start()

    for b in range(SCALE_FIRST, 8):
        scale(b)

    def arrived(dst, sem):
        pltpu.make_async_remote_copy(
            src_ref=total, dst_ref=dst, send_sem=sem, recv_sem=sem, device_id=sibling, device_id_type=MESH
        ).wait_recv()

    def share(b, xx, yy):
        return pltpu.make_async_remote_copy(
            src_ref=zsum.at[b], dst_ref=high.at[b, mine],
            send_sem=hi_send.at[b], recv_sem=hi_recv.at[b],
            device_id=device(xx, yy, c), device_id_type=MESH,
        )

    def spread(b, sources, sems):
        @pl.when(bits[5 + b] == 1)
        def _():
            count = sources.shape[0]
            for n in range(count):
                arrived(sources.at[n], sems.at[n])
            values = [sources[n] for n in range(count)]
            while len(values) > 1:
                values = [values[i] + values[i + 1] for i in range(0, len(values), 2)]
            zsum[b] = values[0]
            for dx, dy in OFFSETS:
                share(b, xs[dx], ys[dy]).start()
            high[b, mine] = values[0]

    sources = ((five, five_recv), (six, six_recv), (zparts, z_recv))
    for b in HIGH_ORDER:
        spread(b, *sources[b])

    def low_forward(b):
        return pltpu.make_async_remote_copy(
            src_ref=low.at[b - 1, half], dst_ref=low.at[b - 1, half],
            send_sem=fw_send.at[2 + b], recv_sem=fw_recv.at[2 + b], device_id=sibling, device_id_type=MESH,
        )

    def high_forward(b):
        return pltpu.make_async_remote_copy(
            src_ref=high.at[b, half], dst_ref=high.at[b, half],
            send_sem=fw_send.at[b], recv_sem=fw_recv.at[b], device_id=sibling, device_id_type=MESH,
        )

    def add(b, matrix):
        for h in range(HEADS):
            acc[:, head(h)] += jnp.dot(
                scaled[b, :, head(h)], matrix(h).reshape(HD, HD).astype(BF16), preferred_element_type=F32
            )

    def straight_wait(slot):
        bytes_of(CHIPS, y_send.at[0], y_recv.at[slot]).wait_recv()

    @pl.when(bits[1] == 1)
    def _():
        straight_wait(0)
        low_forward(1).start()

    @pl.when(bits[2] == 1)
    def _():
        straight_wait(1)
        straight_wait(2)
        low[1, half] = pair[0] + pair[1]
        low_forward(2).start()

    for b in (3, 4):
        @pl.when(bits[b] == 1)
        def _(b=b):
            bytes_of(CHIPS - 1, lo_send.at[b - 3], lo_recv.at[b - 3]).wait_recv()
            low_forward(b).start()

    def high_wait(b):
        @pl.when(bits[5 + b] == 1)
        def _():
            bytes_of(CHIPS - 1, hi_send.at[b], hi_recv.at[b]).wait_recv()
            high_forward(b).start()

    @pl.when(c == 1)
    def _():
        zero_copy.wait_recv()
        add(0, lambda h: (zero if h < 2 else other)[head_chunks(h % 2)])

    def add_low(b):
        @pl.when(bits[b] == 1)
        def _():
            low_forward(b).wait_recv()
            add(b, lambda h: low[b - 1, head_chunks(h)])

    add_low(1)
    add_low(2)
    high_wait(HIGH_ORDER[0])
    add_low(3)
    high_wait(HIGH_ORDER[1])
    add_low(4)
    high_wait(HIGH_ORDER[2])

    for b in HIGH_ORDER:
        @pl.when(bits[5 + b] == 1)
        def _(b=b):
            high_forward(b).wait_recv()
            add(5 + b, lambda h: high[b, head_chunks(h)])

    other_copy.wait_send()
    bytes_of(CHIPS - 1, rs_send, rs_recv).wait_send()

    @pl.when(c == 0)
    def _():
        zero_copy.wait_send()

    for at, steps in enumerate(six_steps):
        @pl.when(place == at)
        def _(steps=steps):
            for step in steps:
                six_copy(step).wait_send()

    @pl.when(bits[5] == 0)
    def _():
        five_copy.wait_send()

    @pl.when(z < 4)
    def _():
        for layer in range(4, 8):
            z_copy(layer).wait_send()

    for at, to, slot in straight:
        @pl.when(y == at)
        def _(to=to, slot=slot):
            straight_copy(to, slot).wait_send()

    for b in (3, 4):
        for bit in range(2):
            @pl.when(bits[b] == bit)
            def _(b=b, bit=bit):
                bytes_of(CHIPS // 2 - bit, lo_send.at[b - 3], lo_recv.at[b - 3]).wait_send()
    for b in range(1, 5):
        @pl.when(bits[b] == 1)
        def _(b=b):
            low_forward(b).wait_send()

    for b in range(3):
        @pl.when(bits[5 + b] == 1)
        def _(b=b):
            high_forward(b).wait_send()
            bytes_of(CHIPS - 1, hi_send.at[b], hi_recv.at[b]).wait_send()


def normalize(x_ref, o_hbm, out, sem):
    copies = []
    for n in range(SPANS):
        rows = slice(n * SPAN, (n + 1) * SPAN)
        for h in range(HEADS):
            cols = slice(h * HD, (h + 1) * HD)
            value = x_ref[rows, cols]
            square = jnp.mean(value * value, axis=-1, keepdims=True)
            out[rows, cols] = (value * lax.rsqrt(square + EPS)).astype(BF16)
        copies.append(pltpu.make_async_copy(out.at[rows], o_hbm.at[rows], sem.at[n]))
        copies[-1].start()
    for copy in copies:
        copy.wait()


def on_device(query_rows, key_rows, value_rows, level_ids, level_table):
    hbm = pl.BlockSpec(memory_space=pltpu.HBM)
    vmem = pl.BlockSpec(memory_space=pltpu.VMEM)
    dma = pltpu.SemaphoreType.DMA
    wide = (TOK, HEADS * HD)
    chunk = (CH, HD)
    unnormed = pl.pallas_call(
        kernel,
        out_shape=jax.ShapeDtypeStruct(wide, F32),
        in_specs=[hbm] * 5,
        out_specs=vmem,
        scratch_shapes=[
            pltpu.VMEM(wide, BF16),
            pltpu.VMEM(wide, BF16),
            pltpu.VMEM(wide, BF16),
            pltpu.VMEM((SPANS, SPAN), jnp.int32),
            pltpu.VMEM((CLASSES, HEADS, LEVELS), F32),
            pltpu.VMEM((CHUNKS, *chunk), F32),
            pltpu.VMEM((CHIPS, *chunk), F32),
            pltpu.VMEM((CHIPS, *chunk), F32),
            pltpu.VMEM((CHIPS, *chunk), F32),
            pltpu.VMEM((3, *chunk), F32),
            pltpu.VMEM(chunk, F32),
            pltpu.VMEM((1, *chunk), F32),
            pltpu.VMEM((2, *chunk), F32),
            pltpu.VMEM((4, *chunk), F32),
            pltpu.VMEM((3, *chunk), F32),
            pltpu.VMEM((CHIPS, *chunk), F32),
            pltpu.VMEM((2, CHIPS, *chunk), F32),
            pltpu.VMEM((4, CHUNKS, *chunk), F32),
            pltpu.VMEM((3, CHUNKS, *chunk), F32),
            pltpu.VMEM((TOK, LEVELS * HEADS), F32),
            pltpu.VMEM((8, *wide), BF16),
            dma((7,)), dma((2,)), dma, dma, dma((2,)), dma((4,)), dma((3,)), dma((2,)), dma((2,)), dma((3,)), dma((3,)),
            dma((7,)), dma((7,)),
            dma((4,)), dma((4,)), dma, dma((1,)), dma((3,)), dma((2,)), pltpu.SemaphoreType.REGULAR((LAYERS,)),
        ],
        compiler_params=pltpu.CompilerParams(
            collective_id=0, has_side_effects=True, vmem_limit_bytes=24 * 2**20
        ),
        name="fenwick",
    )(
        *[
            pltpu.with_memory_space_constraint(a, pltpu.HBM)
            for a in (
                query_rows, key_rows, value_rows,
                level_ids.reshape(SPANS, SPAN), jnp.transpose(level_table, (0, 2, 1)),
            )
        ]
    )
    return pl.pallas_call(
        normalize,
        out_shape=jax.ShapeDtypeStruct(wide, BF16),
        in_specs=[vmem],
        out_specs=hbm,
        scratch_shapes=[pltpu.VMEM(wide, BF16), dma((SPANS,))],
        compiler_params=pltpu.CompilerParams(vmem_limit_bytes=8 * 2**20),
        name="normalize",
    )(unnormed)


def solution(mesh):
    rows = P(("outer", "inner"), None)
    return jax.shard_map(
        on_device, mesh=mesh,
        in_specs=(rows, rows, rows, P(("outer", "inner")), P()),
        out_specs=rows, check_vma=False,
    )
```

time: 26.6 us -> 25.1 us (0.944)
  Pallas kernels: 26.5 us -> 25 us
    pallas_call x1, Pallas kernels: 25.3 us -> 23.9 us  [on_device(): pl.pallas_call(kernel, out_shape=jax.ShapeDtypeStruct(wide, F32), in_spec...]
where the time goes in v4:
time: 25.1 us; the launch traced here: 25 us
  Pallas kernels  25 us (100%)
    pallas_call x1, Pallas kernels, on_device(): pl.pallas_call(kernel, out_shape=jax.ShapeDtypeStruct(wide, F32), in_spec...  23.9 us
    pallas_call x1, Pallas kernels, on_device(): pl.pallas_call(normalize, out_shape=jax.ShapeDtypeStruct(wide, BF16), in_...  1.05 us

profile of v4, /device:TPU:255, one launch (start us, length us, event | category | flops | bytes accessed | tf_op | source)
XLA Modules:
  0.0 25.0 jit_solution(2240793509009913657)
XLA Ops:
  0.0 23.9 %fenwick.1.x_ref = f32[512,512]{1,0:T(8,128)S(1)} custom-call(bf16[512,512]{1,0:T(8,128)(2,1)} %q_hbm.1, bf16[512,512]{1,0:T(8,128)(2,1)} %k_hbm.1, bf16[512,512]{1,0:T(8,128)(2,1)} %v_hbm.1, s32[4,128]{1,0:T(4,128)} %bitcast.3, f32[16,4,16]{2,1,0:T(4,128)} %bitcast.2), custom_call_target="tpu_custom_call" | custom-call | tf_op jit(solution)/shard_map/fenwick/pallas_call | solution.py:458
  23.9 1.0 %normalize.1 = bf16[512,512]{1,0:T(8,128)(2,1)} custom-call(f32[512,512]{1,0:T(8,128)S(1)} %fenwick.1.x_ref), custom_call_target="tpu_custom_call" | custom-call | tf_op jit(solution)/shard_map/normalize/pallas_call | solution.py:502

commit v5 on v4

--- a/solution.py
+++ b/solution.py
@@ -28,14 +28,13 @@
     key=lambda o: -(min(o[0], 4 - o[0]) + min(o[1], 4 - o[1])),
 )
 STEPS = sorted(range(1, LAYERS), key=lambda s: -min(s, LAYERS - s))
-SCALE_FIRST = 4
+SCALE_FIRST = 6
 HIGH_ORDER = (0, 2, 1)
-Y_EARLY = True
 
 
 def kernel(
     q_hbm, k_hbm, v_hbm, ids_hbm, table_hbm, acc,
-    q, k, v, ids, table, state, other, chip_state, parts, sums, total, five, six, zparts, zsum, zero, pair, low, high,
+    q, k, v, ids, table, state, other, chip_state, parts, sums, total, five, six, zparts, zsum, zero, low, high,
     lam, scaled,
     in_sem, other_sem, rs_send, rs_recv, zero_sem, y_send, y_recv, lo_send, lo_recv, hi_send, hi_recv, fw_send, fw_recv,
     z_send, z_recv, five_send, five_recv, six_send, six_recv, ready,
@@ -134,39 +133,29 @@
         to_owner(xs[dx], ys[dy]).start()
     parts[p] = chip_state[p]
 
-    straight = ((0, 3, 1), (1, 3, 2), (0, 2, 1), (1, 2, 2), (0, 1, 0), (2, 3, 0))
-
-    def straight_copy(to, slot):
-        dst = low.at[0, half] if slot == 0 else pair.at[slot - 1]
-        return pltpu.make_async_remote_copy(
-            src_ref=chip_state, dst_ref=dst,
-            send_sem=y_send.at[to], recv_sem=y_recv.at[slot],
-            device_id=device(x, to, c), device_id_type=MESH,
-        )
-
-    def start_straight():
-        for at, to, slot in straight:
-            @pl.when(y == at)
-            def _(to=to, slot=slot):
-                straight_copy(to, slot).start()
-
-    if Y_EARLY:
-        start_straight()
-
-    zero_copy = pltpu.make_async_remote_copy(
-        src_ref=state.at[pl.ds(0, CHIPS)], dst_ref=zero, send_sem=zero_sem.at[0], recv_sem=zero_sem.at[1],
-        device_id=sibling, device_id_type=MESH,
-    )
-
-    @pl.when(c == 0)
-    def _():
-        zero_copy.start()
-
     bits = (
         [c]
         + [lax.rem(lax.div(p, 2**b), 2) for b in range(4)]
         + [lax.rem(lax.div(z, 2**b), 2) for b in range(3)]
     )
+    near_copy = pltpu.make_async_remote_copy(
+        src_ref=chip_state, dst_ref=low.at[0, half], send_sem=y_send, recv_sem=y_recv,
+        device_id=device(x, lax.rem(y + 1, 4), c), device_id_type=MESH,
+    )
+
+    @pl.when(bits[1] == 0)
+    def _():
+        near_copy.start()
+
+    zero_copy = pltpu.make_async_remote_copy(
+        src_ref=state.at[pl.ds(0, CHIPS)], dst_ref=zero, send_sem=zero_sem.at[0], recv_sem=zero_sem.at[1],
+        device_id=sibling, device_id_type=MESH,
+    )
+
+    @pl.when(c == 0)
+    def _():
+        zero_copy.start()
+
     for copy in late_loads:
         copy.wait()
     classes = lax.broadcasted_iota(jnp.int32, (CLASSES, SPAN), 0)
@@ -252,27 +241,28 @@
         pl.semaphore_wait(ready.at[1], 1)
         five_copy.start()
 
-    sums[0], sums[1], sums[2] = groups[2][0], groups[2][2], groups[3][0]
+    for n in range(4):
+        sums[n] = groups[1][2 * n]
+    sums[4], sums[5], sums[6] = groups[2][0], groups[2][2], groups[3][0]
+
+    def low_source(level, xx):
+        return {2: xx, 3: 4 + lax.div(xx, 2), 4: 6}[level]
 
     def low_copy(level, xx, yy):
-        src = sums.at[lax.div(xx, 2)] if level == 3 else sums.at[2]
-        return pltpu.make_async_remote_copy(
-            src_ref=src, dst_ref=low.at[level - 1, mine],
-            send_sem=lo_send.at[level - 3], recv_sem=lo_recv.at[level - 3],
+        return pltpu.make_async_remote_copy(
+            src_ref=sums.at[low_source(level, xx)], dst_ref=low.at[level - 1, mine],
+            send_sem=lo_send.at[level - 2], recv_sem=lo_recv.at[level - 2],
             device_id=device(xx, yy, c), device_id_type=MESH,
         )
 
     for dx, dy in OFFSETS:
         xx, yy = xs[dx], ys[dy]
-        for level, bit in ((3, lax.rem(xx, 2)), (4, lax.div(xx, 2))):
+        for level, bit in ((2, lax.div(yy, 2)), (3, lax.rem(xx, 2)), (4, lax.div(xx, 2))):
             @pl.when(bit == 1)
             def _(level=level, xx=xx, yy=yy):
                 low_copy(level, xx, yy).start()
-    low[2, mine] = sums[lax.div(x, 2)]
-    low[3, mine] = sums[2]
-
-    if not Y_EARLY:
-        start_straight()
+    for level in (2, 3, 4):
+        low[level - 1, mine] = sums[low_source(level, x)]
 
     def z_copy(layer):
         return pltpu.make_async_remote_copy(
@@ -338,25 +328,15 @@
                 scaled[b, :, head(h)], matrix(h).reshape(HD, HD).astype(BF16), preferred_element_type=F32
             )
 
-    def straight_wait(slot):
-        bytes_of(CHIPS, y_send.at[0], y_recv.at[slot]).wait_recv()
-
     @pl.when(bits[1] == 1)
     def _():
-        straight_wait(0)
+        near_copy.wait_recv()
         low_forward(1).start()
 
-    @pl.when(bits[2] == 1)
-    def _():
-        straight_wait(1)
-        straight_wait(2)
-        low[1, half] = pair[0] + pair[1]
-        low_forward(2).start()
-
-    for b in (3, 4):
+    for b in (2, 3, 4):
         @pl.when(bits[b] == 1)
         def _(b=b):
-            bytes_of(CHIPS - 1, lo_send.at[b - 3], lo_recv.at[b - 3]).wait_recv()
+            bytes_of(CHIPS - 1, lo_send.at[b - 2], lo_recv.at[b - 2]).wait_recv()
             low_forward(b).start()
 
     def high_wait(b):
@@ -412,16 +392,15 @@
         for layer in range(4, 8):
             z_copy(layer).wait_send()
 
-    for at, to, slot in straight:
-        @pl.when(y == at)
-        def _(to=to, slot=slot):
-            straight_copy(to, slot).wait_send()
-
-    for b in (3, 4):
+    @pl.when(bits[1] == 0)
+    def _():
+        near_copy.wait_send()
+
+    for b in (2, 3, 4):
         for bit in range(2):
             @pl.when(bits[b] == bit)
             def _(b=b, bit=bit):
-                bytes_of(CHIPS // 2 - bit, lo_send.at[b - 3], lo_recv.at[b - 3]).wait_send()
+                bytes_of(CHIPS // 2 - bit, lo_send.at[b - 2], lo_recv.at[b - 2]).wait_send()
     for b in range(1, 5):
         @pl.when(bits[b] == 1)
         def _(b=b):
@@ -470,19 +449,18 @@
             pltpu.VMEM((CHIPS, *chunk), F32),
             pltpu.VMEM((CHIPS, *chunk), F32),
             pltpu.VMEM((CHIPS, *chunk), F32),
-            pltpu.VMEM((3, *chunk), F32),
+            pltpu.VMEM((7, *chunk), F32),
             pltpu.VMEM(chunk, F32),
             pltpu.VMEM((1, *chunk), F32),
             pltpu.VMEM((2, *chunk), F32),
             pltpu.VMEM((4, *chunk), F32),
             pltpu.VMEM((3, *chunk), F32),
             pltpu.VMEM((CHIPS, *chunk), F32),
-            pltpu.VMEM((2, CHIPS, *chunk), F32),
             pltpu.VMEM((4, CHUNKS, *chunk), F32),
             pltpu.VMEM((3, CHUNKS, *chunk), F32),
             pltpu.VMEM((TOK, LEVELS * HEADS), F32),
             pltpu.VMEM((8, *wide), BF16),
-            dma((7,)), dma((2,)), dma, dma, dma((2,)), dma((4,)), dma((3,)), dma((2,)), dma((2,)), dma((3,)), dma((3,)),
+            dma((7,)), dma((2,)), dma, dma, dma((2,)), dma, dma, dma((3,)), dma((3,)), dma((3,)), dma((3,)),
             dma((7,)), dma((7,)),
             dma((4,)), dma((4,)), dma, dma((1,)), dma((3,)), dma((2,)), pltpu.SemaphoreType.REGULAR((LAYERS,)),
         ],

time: 25.1 us -> 24.6 us (0.980)
  the two profiles are of different devices: /device:TPU:255 before, /device:TPU:225 now
where the time goes in v5:
time: 24.6 us; the launch traced here: 24.5 us
  Pallas kernels  24.5 us (100%)
    pallas_call x1, Pallas kernels, on_device(): pl.pallas_call(kernel, out_shape=jax.ShapeDtypeStruct(wide, F32), in_spec...  23.4 us
    pallas_call x1, Pallas kernels, on_device(): pl.pallas_call(normalize, out_shape=jax.ShapeDtypeStruct(wide, BF16), in_...  1.05 us

profile of v5, /device:TPU:225, one launch (start us, length us, event | category | flops | bytes accessed | tf_op | source)
XLA Modules:
  0.0 24.5 jit_solution(17871543832969787637)
XLA Ops:
  0.0 23.4 %fenwick.1.x_ref = f32[512,512]{1,0:T(8,128)S(1)} custom-call(bf16[512,512]{1,0:T(8,128)(2,1)} %q_hbm.1, bf16[512,512]{1,0:T(8,128)(2,1)} %k_hbm.1, bf16[512,512]{1,0:T(8,128)(2,1)} %v_hbm.1, s32[4,128]{1,0:T(4,128)} %bitcast.3, f32[16,4,16]{2,1,0:T(4,128)} %bitcast.2), custom_call_target="tpu_custom_call" | custom-call | tf_op jit(solution)/shard_map/fenwick/pallas_call | solution.py:437
  23.4 1.0 %normalize.1 = bf16[512,512]{1,0:T(8,128)(2,1)} custom-call(f32[512,512]{1,0:T(8,128)S(1)} %fenwick.1.x_ref), custom_call_target="tpu_custom_call" | custom-call | tf_op jit(solution)/shard_map/normalize/pallas_call | solution.py:480

commit v6 on v5

--- a/solution.py
+++ b/solution.py
@@ -71,7 +71,7 @@
         for n, cc in enumerate((1 - c, c))
     ]
     late_loads = [load(ids_hbm, ids, 4), load(table_hbm, table, 5), load(q_hbm, q, 6)]
-    for copy in key_loads[0] + key_loads[1] + late_loads:
+    for copy in key_loads[0]:
         copy.start()
 
     barrier = pltpu.get_barrier_semaphore()
@@ -104,6 +104,8 @@
             value = contract_tokens(k[:, cols], v[:, cols])
             state[pl.ds(cc * CHIPS + i * PER_HEAD, PER_HEAD)] = value.reshape(PER_HEAD, CH, HD)
 
+    for copy in key_loads[1]:
+        copy.start()
     half_state(0, 1 - c)
     pl.semaphore_wait(barrier, CHIPS - 1 + 1 + z)
     half, other_half = pl.ds(c * CHIPS, CHIPS), pl.ds((1 - c) * CHIPS, CHIPS)
@@ -112,12 +114,14 @@
         send_sem=other_sem.at[0], recv_sem=other_sem.at[1], device_id=sibling, device_id_type=MESH,
     )
     other_copy.start()
-    half_state(1, c)
-
+    for copy in late_loads:
+        copy.start()
     for step in STEPS:
         @pl.when(step <= z)
         def _(step=step):
             pl.semaphore_signal(ready.at[step], inc=1, device_id=in_layer(z - step), device_id_type=MESH)
+
+    half_state(1, c)
 
     other_copy.wait_recv()
     chip_state[...] = state[half] + other[...]
@@ -202,6 +206,17 @@
     for b in range(SCALE_FIRST):
         scale(b)
 
+    def add(b, matrix):
+        for h in range(HEADS):
+            acc[:, head(h)] += jnp.dot(
+                scaled[b, :, head(h)], matrix(h).reshape(HD, HD).astype(BF16), preferred_element_type=F32
+            )
+
+    @pl.when(c == 1)
+    def _():
+        zero_copy.wait_recv()
+        add(0, lambda h: (zero if h < 2 else other)[head_chunks(h % 2)])
+
     def bytes_of(n, send_sem, recv_sem):
         return pltpu.make_async_remote_copy(
             src_ref=state.at[pl.ds(0, n)], dst_ref=state.at[pl.ds(0, n)],
@@ -322,12 +337,6 @@
             send_sem=fw_send.at[b], recv_sem=fw_recv.at[b], device_id=sibling, device_id_type=MESH,
         )
 
-    def add(b, matrix):
-        for h in range(HEADS):
-            acc[:, head(h)] += jnp.dot(
-                scaled[b, :, head(h)], matrix(h).reshape(HD, HD).astype(BF16), preferred_element_type=F32
-            )
-
     @pl.when(bits[1] == 1)
     def _():
         near_copy.wait_recv()
@@ -344,11 +353,6 @@
         def _():
             bytes_of(CHIPS - 1, hi_send.at[b], hi_recv.at[b]).wait_recv()
             high_forward(b).start()
-
-    @pl.when(c == 1)
-    def _():
-        zero_copy.wait_recv()
-        add(0, lambda h: (zero if h < 2 else other)[head_chunks(h % 2)])
 
     def add_low(b):
         @pl.when(bits[b] == 1)

time: 24.6 us -> 24.6 us (level)
  no operation moved by 1% of the time
where the time goes in v6:
time: 24.6 us; the launch traced here: 24.5 us
  Pallas kernels  24.4 us (99%)
    pallas_call x1, Pallas kernels, on_device(): pl.pallas_call(kernel, out_shape=jax.ShapeDtypeStruct(wide, F32), in_spec...  23.4 us
    pallas_call x1, Pallas kernels, on_device(): pl.pallas_call(normalize, out_shape=jax.ShapeDtypeStruct(wide, BF16), in_...  1.05 us

profile of v6, /device:TPU:225, one launch (start us, length us, event | category | flops | bytes accessed | tf_op | source)
XLA Modules:
  0.0 24.5 jit_solution(3759836413230231138)
XLA Ops:
  0.0 23.4 %fenwick.1.x_ref = f32[512,512]{1,0:T(8,128)S(1)} custom-call(bf16[512,512]{1,0:T(8,128)(2,1)} %q_hbm.1, bf16[512,512]{1,0:T(8,128)(2,1)} %k_hbm.1, bf16[512,512]{1,0:T(8,128)(2,1)} %v_hbm.1, s32[4,128]{1,0:T(4,128)} %bitcast.3, f32[16,4,16]{2,1,0:T(4,128)} %bitcast.2), custom_call_target="tpu_custom_call" | custom-call | tf_op jit(solution)/shard_map/fenwick/pallas_call | solution.py:441
  23.4 1.0 %normalize.1 = bf16[512,512]{1,0:T(8,128)(2,1)} custom-call(f32[512,512]{1,0:T(8,128)S(1)} %fenwick.1.x_ref), custom_call_target="tpu_custom_call" | custom-call | tf_op jit(solution)/shard_map/normalize/pallas_call | solution.py:484

commit v7 on v5

--- a/solution.py
+++ b/solution.py
@@ -96,22 +96,29 @@
     def contract_tokens(a, b):
         return lax.dot_general(a, b, (((0,), (0,)), ((), ())), preferred_element_type=F32)
 
-    def half_state(n, cc):
+    def half_state(n, cc, sends=()):
         for copy in key_loads[n]:
             copy.wait()
         for i in range(HEADS // 2):
             cols = pl.ds(pl.multiple_of(cc * HALF + i * HD, HD), HD)
             value = contract_tokens(k[:, cols], v[:, cols])
             state[pl.ds(cc * CHIPS + i * PER_HEAD, PER_HEAD)] = value.reshape(PER_HEAD, CH, HD)
-
-    half_state(0, 1 - c)
-    pl.semaphore_wait(barrier, CHIPS - 1 + 1 + z)
-    half, other_half = pl.ds(c * CHIPS, CHIPS), pl.ds((1 - c) * CHIPS, CHIPS)
-    other_copy = pltpu.make_async_remote_copy(
-        src_ref=state.at[other_half], dst_ref=other,
-        send_sem=other_sem.at[0], recv_sem=other_sem.at[1], device_id=sibling, device_id_type=MESH,
-    )
-    other_copy.start()
+            if sends:
+                if i == 0:
+                    pl.semaphore_wait(barrier, CHIPS - 1 + 1 + z)
+                sends[i].start()
+
+    half = pl.ds(c * CHIPS, CHIPS)
+    other_copies = [
+        pltpu.make_async_remote_copy(
+            src_ref=state.at[pl.ds((1 - c) * CHIPS + i * PER_HEAD, PER_HEAD)],
+            dst_ref=other.at[pl.ds(i * PER_HEAD, PER_HEAD)],
+            send_sem=other_sem.at[2 * i], recv_sem=other_sem.at[2 * i + 1],
+            device_id=sibling, device_id_type=MESH,
+        )
+        for i in range(HEADS // 2)
+    ]
+    half_state(0, 1 - c, other_copies)
     half_state(1, c)
 
     for step in STEPS:
@@ -119,7 +126,8 @@
         def _(step=step):
             pl.semaphore_signal(ready.at[step], inc=1, device_id=in_layer(z - step), device_id_type=MESH)
 
-    other_copy.wait_recv()
+    for copy in other_copies:
+        copy.wait_recv()
     chip_state[...] = state[half] + other[...]
 
     def to_owner(xx, yy):
@@ -370,7 +378,8 @@
             high_forward(b).wait_recv()
             add(5 + b, lambda h: high[b, head_chunks(h)])
 
-    other_copy.wait_send()
+    for copy in other_copies:
+        copy.wait_send()
     bytes_of(CHIPS - 1, rs_send, rs_recv).wait_send()
 
     @pl.when(c == 0)
@@ -460,7 +469,7 @@
             pltpu.VMEM((3, CHUNKS, *chunk), F32),
             pltpu.VMEM((TOK, LEVELS * HEADS), F32),
             pltpu.VMEM((8, *wide), BF16),
-            dma((7,)), dma((2,)), dma, dma, dma((2,)), dma, dma, dma((3,)), dma((3,)), dma((3,)), dma((3,)),
+            dma((7,)), dma((4,)), dma, dma, dma((2,)), dma, dma, dma((3,)), dma((3,)), dma((3,)), dma((3,)),
             dma((7,)), dma((7,)),
             dma((4,)), dma((4,)), dma, dma((1,)), dma((3,)), dma((2,)), pltpu.SemaphoreType.REGULAR((LAYERS,)),
         ],

time: 24.6 us -> 24.8 us (level)
    pallas_call x1, Pallas kernels: 23.4 us -> 23.7 us  [on_device(): pl.pallas_call(kernel, out_shape=jax.ShapeDtypeStruct(wide, F32), in_spec...]
where the time goes in v7:
time: 24.8 us; the launch traced here: 24.7 us
  Pallas kernels  24.7 us (100%)
    pallas_call x1, Pallas kernels, on_device(): pl.pallas_call(kernel, out_shape=jax.ShapeDtypeStruct(wide, F32), in_spec...  23.7 us
    pallas_call x1, Pallas kernels, on_device(): pl.pallas_call(normalize, out_shape=jax.ShapeDtypeStruct(wide, BF16), in_...  1.05 us

profile of v7, /device:TPU:225, one launch (start us, length us, event | category | flops | bytes accessed | tf_op | source)
XLA Modules:
  0.0 24.7 jit_solution(15577405687459813298)
XLA Ops:
  0.0 23.7 %fenwick.1.x_ref = f32[512,512]{1,0:T(8,128)S(1)} custom-call(bf16[512,512]{1,0:T(8,128)(2,1)} %q_hbm.1, bf16[512,512]{1,0:T(8,128)(2,1)} %k_hbm.1, bf16[512,512]{1,0:T(8,128)(2,1)} %v_hbm.1, s32[4,128]{1,0:T(4,128)} %bitcast.3, f32[16,4,16]{2,1,0:T(4,128)} %bitcast.2), custom_call_target="tpu_custom_call" | custom-call | tf_op jit(solution)/shard_map/fenwick/pallas_call | solution.py:446
  23.7 1.0 %normalize.1 = bf16[512,512]{1,0:T(8,128)(2,1)} custom-call(f32[512,512]{1,0:T(8,128)S(1)} %fenwick.1.x_ref), custom_call_target="tpu_custom_call" | custom-call | tf_op jit(solution)/shard_map/normalize/pallas_call | solution.py:489
